TPU v7x, 32 devices: a whole 2x2x4 slice. The times are simulated.
32 devices in a mesh: tm: 8 (over z, y), order: 4 (over x, core).
Axes of the slice: x: 2, y: 2, z: 4, core: 2. Of those that a mesh axis runs over, the one named last changes fastest.
Arguments:
- longitude: float32 [32768], P('tm'), may hold values from -3.140625 to 3.140625
- node_index: int32 [32768], P('tm'), may hold values from 0 to 159
- weight: float32 [32768], P('tm'), may hold values from 0.5 to 2
- gradient: float32 [32768], P('tm'), may hold values from 2 to 6
- segment: int32 [32768], P('tm'), may hold values from 0 to 31, never falling along the last dimension, each value on 1 to 4096 neighbouring positions
- order_map: int32 [304], P('order'), may hold values from 0 to 303, each once
- legendre: bfloat16 [304, 160, 304], P('order'), may hold values from -0.0625 to 0.0625
- precond: float32 [19, 2, 304, 304], P(None, None, 'order'), may hold values from 0 to 1, as said below
- kaula_prior: float32 [2, 304, 304], P(None, 'order'), may hold values from 0.5 to 5
- start_iterate: float32 [2, 304, 304], P(None, 'order'), may hold values from -6 to 6
- direction: float32 [2, 304, 304], P(None, 'order'), may hold values from -6 to 6
Outputs:
- iterate: float32 [2, 304, 304], P(None, 'order')
- residual: float32 [2, 304, 304], P(None, 'order')
- new_direction: float32 [2, 304, 304], P(None, 'order')
Inputs may be any that keep to these rules, and one draw needn't show every extreme that they name: `precond`: each block of 19 degrees is a symmetric positive definite matrix.
All inputs are finite; a program needn't handle non-finite values.
Results may differ from a plain program's by a relative error of at most 0.0003.
Values sent between devices are 32-bit elements; how exact they have to be, the bound alone decides.
No kernel may reach another device: no remote copies, remote signals or barrier semaphores. Data moves between devices by JAX's collectives and lax.ppermute only.
A program may use at most 128 MiB of HBM per device.

v0:
```python
import jax
import jax.numpy as jnp
from jax import lax
from jax.sharding import PartitionSpec as P

LMAX = 300
DB = 19
ITERS = 2


def extended(x, sides, width):
    for axis, dim in sides:
        size, length = (lax.axis_size(axis), x.shape[dim])
        up = [(i, (i + 1) % size) for i in range(size - 1)]
        down = [(j, i) for i, j in up]
        last = lax.slice_in_dim(x, length - width, length, axis=dim)
        leading = lax.slice_in_dim(x, 0, width, axis=dim)
        before = lax.ppermute(last, axis, up)
        after = lax.ppermute(leading, axis, down)
        x = jnp.concatenate([before, x, after], axis=dim)
    return x


def valid_mask_of(order_map, degrees):
    order_ids = order_map[None, :, None]
    degree_ids = jnp.arange(degrees, dtype=jnp.int32)[None, None, :]
    part_ids = jnp.arange(2, dtype=jnp.int32)[:, None, None]
    keep = (
        (degree_ids <= LMAX)
        & (degree_ids >= jnp.maximum(order_ids, 2))
        & ((part_ids == 0) | (order_ids >= 1))
    )
    return keep.astype(jnp.float32)


def make_phase(longitude, order_map):
    angle = longitude[:, None] * order_map.astype(jnp.float32)[None, :]
    return jnp.concatenate([jnp.cos(angle), jnp.sin(angle)], axis=1)


def precondition(blocks, vector):
    flat = vector.reshape(-1)
    block_count = flat.shape[0] // DB
    shaped = blocks.reshape(DB, block_count, DB)
    result = jnp.einsum(
        "jbi,bj->bi", shaped, flat.reshape(block_count, DB), precision=lax.Precision.HIGHEST
    )
    return result.reshape(vector.shape)


def run_steps(
    residual,
    iterate,
    new_direction,
    valid_mask,
    kaula_prior,
    precond,
    image_sum,
    pair_sum,
    single_sum,
):
    for iteration in range(ITERS):
        image = valid_mask * (kaula_prior * new_direction - image_sum(new_direction))
        residual_dot, curvature = pair_sum(
            jnp.sum(residual * new_direction), jnp.sum(new_direction * image)
        )
        step_size = residual_dot / curvature
        iterate = iterate + step_size * new_direction
        residual = residual - step_size * image
        smoothed = valid_mask * precondition(precond, residual)
        conj_dot = single_sum(jnp.sum(smoothed * image))
        new_direction = smoothed - conj_dot / curvature * new_direction
    return (iterate, residual, new_direction)


def shards(
    longitude,
    node_index,
    weight,
    gradient,
    segment,
    order_map,
    legendre,
    precond,
    kaula_prior,
    start_iterate,
    direction,
):
    row_count = longitude.shape[0]
    slot_count, node_count, degrees = legendre.shape
    valid_mask = valid_mask_of(order_map, degrees)
    selector = (jnp.arange(node_count, dtype=jnp.int32)[:, None] == node_index[None, :]).astype(
        jnp.float32
    )
    first_id = segment[0]
    last_id = segment[-1]
    offset = segment - first_id
    tail_index = last_id - first_id
    weight_sums = jax.ops.segment_sum(weight, offset, num_segments=row_count)
    edge_stats = jnp.stack(
        [
            jnp.stack([first_id, last_id]).astype(jnp.float32) + 1.0,
            jnp.stack([weight_sums[0], weight_sums[tail_index]]),
        ]
    )
    padded = extended(edge_stats, (("tm", 1),), 1)
    join_prev = (padded[0, 0] == edge_stats[0, 0]).astype(jnp.float32)
    join_next = (padded[0, 3] == edge_stats[0, 1]).astype(jnp.float32)
    weight_sums = (
        weight_sums.at[0].add(join_prev * padded[1, 0]).at[tail_index].add(join_next * padded[1, 3])
    )
    weight_sums = jnp.where(weight_sums > 0.0, weight_sums, 1.0)

    def center_rows(values):
        value_sums = jax.ops.segment_sum(weight * values, offset, num_segments=row_count)
        edge_sums = jnp.stack([value_sums[0], value_sums[tail_index]])
        beside_all = extended(edge_sums, (("tm", 0),), 1)
        value_sums = (
            value_sums.at[0]
            .add(join_prev * beside_all[0])
            .at[tail_index]
            .add(join_next * beside_all[3])
        )
        return weight * (values - jnp.take(value_sums / weight_sums, offset))

    stored_table = make_phase(longitude, order_map)

    def phases():
        return stored_table

    def node_part(vector, observed):
        nodal = jnp.einsum(
            "mkn,cmn->kcm", legendre.astype(jnp.float32), vector, precision=lax.Precision.HIGHEST
        ).reshape(node_count, 2 * slot_count)
        row_terms = lax.dot_general(
            selector, nodal, (((0,), (0,)), ((), ())), precision=lax.Precision.HIGHEST
        )
        partial_rows = jnp.sum(row_terms * phases(), axis=1)
        predicted = lax.psum(partial_rows, "order")
        centered = center_rows(observed - predicted)
        node_terms = jnp.dot(
            selector, phases() * centered[:, None], precision=lax.Precision.HIGHEST
        )
        return node_terms.reshape(node_count, 2, slot_count)

    def lifted(node_terms):
        return jnp.einsum(
            "mkn,kcm->cmn",
            legendre.astype(jnp.float32),
            node_terms,
            precision=lax.Precision.HIGHEST,
        )

    no_data = jnp.zeros_like(gradient)
    iterate = start_iterate * valid_mask
    new_direction = direction * valid_mask

    def summed(vector, observed):
        return lifted(lax.psum(node_part(vector, observed), "tm"))

    def pair_sum(first, second):
        return lax.psum((first, second), "order")

    def single_sum(value):
        return lax.psum(value, "order")

    residual = valid_mask * (summed(iterate, gradient) - kaula_prior * iterate)
    return run_steps(
        residual,
        iterate,
        new_direction,
        valid_mask,
        kaula_prior,
        precond,
        lambda vector: summed(vector, no_data),
        pair_sum,
        single_sum,
    )


def solution(mesh):
    placed = (
        P("tm"),
        P("tm"),
        P("tm"),
        P("tm"),
        P("tm"),
        P("order"),
        P("order", None, None),
        P(None, None, "order", None),
        P(None, "order", None),
        P(None, "order", None),
        P(None, "order", None),
    )
    return jax.shard_map(
        shards,
        mesh=mesh,
        in_specs=placed,
        out_specs=(P(None, "order", None), P(None, "order", None), P(None, "order", None)),
        check_vma=False,
    )
```

profile of v0, /device:TPU:0, one launch (start us, length us, event | category | flops | bytes accessed | tf_op | source)
XLA Modules:
  0.0 635.9 jit_solution(18027174269071761478)
XLA Ops:
  12.5 29.0 %scatter_custom_fusion.1 = f32[4096]{0:T(1024)S(1)} fusion(s32[4096]{0:T(1024)S(1)} %get-tuple-element.117, f32[4096]{0:T(1024)} %param.31, f32[]{:T(128)} %constant.182.clone.1), kind=kCustom, calls=%fused_computation.86 | custom fusion | flops 4096 | bytes 16896 | tf_op jit(solution)/shard_map/scatter-add | solution.py:99
  44.9 5.5 collective-permute-start
  52.0 12.4 %convolution_bitcast_fusion.4 = f32[160,2,76]{0,1,2:T(2,128)S(1)} fusion(bf16[76,160,304]{2,1,0:T(8,128)(2,1)} %param.35, f32[2,76,304]{2,0,1:T(2,128)} %param.39, pred[2,76]{0,1:T(8,128)(4,1)S(1)} %broadcast_or_fusion, pred[76,304]{1,0:T(8,128)(4,1)S(1)} %fusion.28), kind=kOutput, calls=%fused_computation.46 | convolution fusion | flops 88811776 | bytes 7698648 | tf_op jit(solution)/shard_map/mkn,cmn->kcm/dot_general | solution.py:132
  64.4 12.7 %convolution_bitcast_fusion.5 = f32[160,2,76]{0,1,2:T(2,128)S(1)} fusion(bf16[76,160,304]{2,1,0:T(8,128)(2,1)} %param.35, f32[2,76,304]{2,0,1:T(2,128)S(1)} %copy-done.5, pred[2,76]{0,1:T(8,128)(4,1)S(1)} %broadcast_or_fusion, pred[76,304]{1,0:T(8,128)(4,1)S(1)} %fusion.28), kind=kOutput, calls=%fused_computation.47 | convolution fusion | flops 88811776 | bytes 7698648 | tf_op jit(solution)/shard_map/mkn,cmn->kcm/dot_general | solution.py:132
  77.9 4.6 multiply_cosine_fusion
  85.6 11.0 %all-reduce.3 = (f32[4096]{0:T(1024)S(1)}, f32[4096]{0:T(1024)S(1)}) all-reduce(f32[4096]{0:T(1024)S(1)} %fusion.11, f32[4096]{0:T(1024)S(1)} %fusion.10), channel_id=1, replica_groups=mesh['tm'=8,'order'=4] {'order'}, use_global_device_ids=true, to_apply=%region_8.10 | all-reduce | flops 8192 | bytes 65536 | tf_op jit(solution)/shard_map/psum | solution.py:139
  96.6 28.8 %scatter_custom_fusion = f32[4096]{0:T(1024)S(1)} fusion(s32[4096]{0:T(1024)S(1)} %get-tuple-element.117, f32[4096]{0:T(1024)S(1)} %get-tuple-element.114, f32[]{:T(128)} %constant.182.clone.1), kind=kCustom, calls=%fused_computation.88 | custom fusion | flops 4096 | bytes 16388 | tf_op jit(solution)/shard_map/scatter-add | solution.py:115
  126.0 4.8 collective-permute-start.1
  130.9 28.8 %scatter_custom_fusion.2 = f32[4096]{0:T(1024)S(1)} fusion(s32[4096]{0:T(1024)S(1)} %get-tuple-element.117, f32[4096]{0:T(1024)S(1)} %get-tuple-element.128, f32[]{:T(128)} %constant.182.clone.1), kind=kCustom, calls=%fused_computation.84 | custom fusion | flops 4096 | bytes 16388 | tf_op jit(solution)/shard_map/scatter-add | solution.py:115
  176.8 23.2 %gather_fusion.1 = f32[4096]{0:T(1024)S(1)} fusion(f32[4096]{0:T(1024)S(1)} %get-tuple-element.124, s32[4096]{0:T(1024)S(1)} %get-tuple-element.116), kind=kCustom, calls=%fused_computation.1.clone | custom fusion | bytes 49152 | tf_op jit(solution)/shard_map/jit(_take)/gather | solution.py:124
  200.0 23.0 %gather_fusion = f32[4096]{0:T(1024)S(1)} fusion(f32[4096]{0:T(1024)S(1)} %get-tuple-element.125, s32[4096]{0:T(1024)S(1)} %get-tuple-element.116), kind=kCustom, calls=%fused_computation.clone | custom fusion | bytes 49152 | tf_op jit(solution)/shard_map/jit(_take)/gather | solution.py:124
  228.5 5.0 copy.22
  233.5 17.6 %reshape.343 = f32[19,2432,19]{2,1,0:T(8,128)} reshape(f32[19,2,76,304]{3,2,1,0:T(8,128)} %copy.22) | data formatting | bytes 7023616 | tf_op jit(solution)/shard_map/reshape | solution.py:44
  251.1 50.9 %all-reduce.9.cloned.1.call-done = (f32[160,2,76]{0,1,2:T(2,128)}, f32[160,2,76]{0,1,2:T(2,128)}) async-done(((f32[160,2,76]{0,1,2:T(2,128)}, f32[160,2,76]{0,1,2:T(2,128)}), (f32[160,2,76]{0,1,2:T(2,128)}, f32[160,2,76]{0,1,2:T(2,128)})) %all-reduce.9.cloned.1.call-update) | async-done | bytes 194576 | tf_op jit(solution)/shard_map/psum | solution.py:159
  302.1 8.2 %fusion.27 = f32[2,76,304]{2,0,1:T(2,128)S(1)} fusion(f32[160,2,76]{0,1,2:T(2,128)} %get-tuple-element.105, bf16[76,160,304]{2,1,0:T(8,128)(2,1)} %param.35, f32[2,76,304]{2,0,1:T(2,128)S(1)} %copy-done.11, pred[2,76]{0,1:T(8,128)(4,1)S(1)} %broadcast_or_fusion, pred[76,304]{1,0:T(8,128)(4,1)S(1)} %fusion.28, f32[2,76,304]{2,0,1:T(2,128)S(1)} %copy-done.5), kind=kOutput, calls=%fused_computation.44 | convolution fusion | flops 88950400 | bytes 8068312 | tf_op jit(solution)/shard_map/mkn,kcm->cmn/dot_general | solution.py:147
  310.3 8.1 %multiply_reduce_fusion.4 = (f32[]{:T(128)}, f32[]{:T(128)}, f32[2,76,304]{2,0,1:T(2,128)S(1)}) fusion(f32[2,76,304]{2,0,1:T(2,128)S(1)} %copy-done, pred[2,76]{0,1:T(8,128)(4,1)S(1)} %broadcast_or_fusion, pred[76,304]{1,0:T(8,128)(4,1)S(1)} %fusion.28, f32[2,76,304]{2,0,1:T(2,128)S(1)} %fusion.27, f32[160,2,76]{0,1,2:T(2,128)S(1)} %copy-done.13, ...), kind=kOutput, calls=%fused_computation.61 | convolution fusion | flops 89135232 | bytes 8253152 | tf_op jit(solution)/shard_map/mkn,kcm->cmn/dot_general | solution.py:147
  318.3 6.3 all-reduce.2
  326.8 49.5 %fusion.2 = f32[2432,1,19]{2,1,0:T(1,128)S(1)} fusion(f32[2432,19,1]{1,2,0:T(1,128)S(1)} %bitcast.90, f32[19,2432,19]{2,1,0:T(8,128)} %reshape.343), kind=kOutput, calls=%fused_computation.9 | convolution fusion | flops 10535424 | bytes 3881472 | tf_op jit(solution)/shard_map/jbi,bj->bi/dot_general | solution.py:45
  377.9 7.2 %psum.90 = f32[]{:T(128)} all-reduce(f32[]{:T(128)} %multiply_reduce_fusion.3), channel_id=1, replica_groups=mesh['tm'=8,'order'=4] {'order'}, use_global_device_ids=true, to_apply=%region_14.16 | all-reduce | flops 1 | bytes 8 | tf_op jit(solution)/shard_map/psum | solution.py:165
  386.7 12.2 %convolution_bitcast_fusion.3 = f32[160,2,76]{0,1,2:T(2,128)S(1)} fusion(f32[2,76,304]{2,0,1:T(2,128)S(1)} %multiply_subtract_fusion.2, bf16[76,160,304]{2,1,0:T(8,128)(2,1)} %param.35), kind=kOutput, calls=%fused_computation.45 | convolution fusion | flops 88719360 | bytes 7675392 | tf_op jit(solution)/shard_map/mkn,cmn->kcm/dot_general | solution.py:132
  399.0 2.8 fusion.12
  401.9 10.2 %psum.92 = f32[4096]{0:T(1024)S(1)} all-reduce(f32[4096]{0:T(1024)S(1)} %fusion.12), channel_id=1, replica_groups=mesh['tm'=8,'order'=4] {'order'}, use_global_device_ids=true, to_apply=%region_18.20 | all-reduce | flops 4096 | bytes 32768 | tf_op jit(solution)/shard_map/psum | solution.py:139
  412.1 28.8 %scatter_custom_fusion.3 = f32[4096]{0:T(1024)S(1)} fusion(s32[4096]{0:T(1024)S(1)} %get-tuple-element.117, f32[4096]{0:T(1024)S(1)} %subtract_multiply_fusion, f32[]{:T(128)} %constant.182.clone.1), kind=kCustom, calls=%fused_computation.82 | custom fusion | flops 4096 | bytes 16388 | tf_op jit(solution)/shard_map/scatter-add | solution.py:115
  441.5 3.1 collective-permute-start.6
  448.0 4.5 collective-permute-done.7
  453.4 23.0 %gather_fusion.2 = f32[4096]{0:T(1024)S(1)} fusion(f32[4096]{0:T(1024)S(1)} %fusion.33, s32[4096]{0:T(1024)S(1)} %get-tuple-element.116), kind=kCustom, calls=%fused_computation.2.clone | custom fusion | bytes 49152 | tf_op jit(solution)/shard_map/jit(_take)/gather | solution.py:124
  476.4 3.2 fusion.4
  480.5 70.8 %all-reduce.7.cloned.1.call-done = f32[160,2,76]{0,1,2:T(2,128)} async-done(((f32[160,2,76]{0,1,2:T(2,128)}), f32[160,2,76]{0,1,2:T(2,128)}) %all-reduce.7.cloned.1.call-update) | async-done | bytes 97296 | tf_op jit(solution)/shard_map/psum | solution.py:159
  551.3 8.8 %multiply_reduce_fusion.1 = (f32[]{:T(128)}, f32[]{:T(128)}, f32[2,76,304]{2,0,1:T(2,128)S(1)}) fusion(f32[2,76,304]{2,0,1:T(2,128)S(1)} %multiply_subtract_fusion.2, f32[2,76,304]{2,0,1:T(2,128)S(1)} %bitcast.93, f32[160,2,76]{0,1,2:T(2,128)} %all-reduce.7.cloned.1.call-done, bf16[76,160,304]{2,1,0:T(8,128)(2,1)} %param.35, ...), kind=kOutput, calls=%fused_computation.56 | convolution fusion | flops 89089024 | bytes 8253152 | tf_op jit(solution)/shard_map/mkn,kcm->cmn/dot_general | solution.py:147
  560.0 6.3 all-reduce.1
  568.5 48.9 %fusion = f32[2432,1,19]{2,1,0:T(1,128)S(1)} fusion(f32[2432,19,1]{1,2,0:T(1,128)S(1)} %bitcast.88, f32[19,2432,19]{2,1,0:T(8,128)} %reshape.343), kind=kOutput, calls=%fused_computation.7 | convolution fusion | flops 10535424 | bytes 3881472 | tf_op jit(solution)/shard_map/jbi,bj->bi/dot_general | solution.py:45
  619.1 7.2 %psum.95 = f32[]{:T(128)} all-reduce(f32[]{:T(128)} %multiply_reduce_fusion), channel_id=1, replica_groups=mesh['tm'=8,'order'=4] {'order'}, use_global_device_ids=true, to_apply=%region_24.26 | all-reduce | flops 1 | bytes 8 | tf_op jit(solution)/shard_map/psum | solution.py:165
  (108 shorter events, 40.3 us)
Async XLA Ops:
  7.2 294.9 %all-reduce.9.cloned.1.call-start = ((), (), s32[]{:S(2)}) async-start(), calls=%async_computation.1 | async-start | bytes 622592 | tf_op jit(solution)/shard_map/psum | solution.py:159
  43.6 127.2 %collective-permute-start.2 = (f32[2,1]{1,0:T(2,128)S(1)}, f32[2,1]{1,0:T(2,128)S(1)}, u32[]{:S(2)}, u32[]{:S(2)}) collective-permute-start(f32[2,1]{1,0:T(2,128)S(1)} %get-tuple-element.139), channel_id=1, source_target_pairs={{4,0},{8,4},{12,8},{16,12},{20,16},{24,20},{28,24},{5,1},{9,5},{13... | collective-permute-start | bytes 32 | tf_op jit(solution)/shard_map/ppermute | solution.py:19
  44.9 118.6 %collective-permute-start = (f32[2,1]{1,0:T(2,128)S(1)}, f32[2,1]{1,0:T(2,128)S(1)}, u32[]{:S(2)}, u32[]{:S(2)}) collective-permute-start(f32[2,1]{1,0:T(2,128)S(1)} %get-tuple-element.140), channel_id=1, source_target_pairs={{0,4},{4,8},{8,12},{12,16},{16,20},{20,24},{24,28},{1,5},{5,9},{9,... | collective-permute-start | bytes 32 | tf_op jit(solution)/shard_map/ppermute | solution.py:18
  52.0 12.4 %copy-start.5 = (f32[2,76,304]{2,0,1:T(2,128)S(1)}, f32[2,76,304]{2,0,1:T(2,128)}, u32[]{:S(2)}) copy-start(f32[2,76,304]{2,0,1:T(2,128)} %param.38) | copy-start | bytes 554500
  64.4 13.5 %copy-start.9 = (f32[4096]{0:T(1024)S(1)}, f32[4096]{0:T(1024)}, u32[]{:S(2)}) copy-start(f32[4096]{0:T(1024)} %param.29) | copy-start | bytes 49156
  77.2 5.3 copy-start.14
  82.5 143.2 %copy-start.1 = (f32[4096,76]{0,1:T(8,128)}, f32[4096,76]{0,1:T(8,128)S(1)}, u32[]{:S(2)}) copy-start(f32[4096,76]{0,1:T(8,128)S(1)} %get-tuple-element.120) | copy-start | bytes 3735556
  82.5 143.2 %copy-start.3 = (f32[4096,76]{0,1:T(8,128)}, f32[4096,76]{0,1:T(8,128)S(1)}, u32[]{:S(2)}) copy-start(f32[4096,76]{0,1:T(8,128)S(1)} %get-tuple-element.121) | copy-start | bytes 3735556
  82.5 1.5 copy-start.8
  84.0 12.6 %copy-start.7 = (f32[4096]{0:T(1024)S(1)}, f32[4096]{0:T(1024)}, u32[]{:S(2)}) copy-start(f32[4096]{0:T(1024)} %param.31) | copy-start | bytes 49156
  84.0 12.6 %copy-start.10 = (f32[4096]{0:T(1024)S(1)}, f32[4096]{0:T(1024)}, u32[]{:S(2)}) copy-start(f32[4096]{0:T(1024)} %param.32) | copy-start | bytes 49156
  126.0 39.9 %collective-permute-start.1 = (f32[1]{0:T(128)}, f32[1]{0:T(128)}, u32[]{:S(2)}, u32[]{:S(2)}) collective-permute-start(f32[1]{0:T(128)} %dynamic_slice.13), channel_id=1, source_target_pairs={{0,4},{4,8},{8,12},{12,16},{16,20},{20,24},{24,28},{1,5},{5,9},{9,... | collective-permute-start | bytes 20 | tf_op jit(solution)/shard_map/ppermute | solution.py:18
  160.3 8.0 %collective-permute-start.4 = (f32[1]{0:T(128)}, f32[1]{0:T(128)}, u32[]{:S(2)}, u32[]{:S(2)}) collective-permute-start(f32[1]{0:T(128)} %dynamic_slice.14), channel_id=1, source_target_pairs={{0,4},{4,8},{8,12},{12,16},{16,20},{20,24},{24,28},{1,5},{5,9},{9,... | collective-permute-start | bytes 20 | tf_op jit(solution)/shard_map/ppermute | solution.py:18
  167.0 6.4 %collective-permute-start.3 = (f32[1]{0:T(128)}, f32[1]{0:T(128)}, u32[]{:S(2)}, u32[]{:S(2)}) collective-permute-start(f32[1]{0:T(128)} %get-tuple-element.129), channel_id=1, source_target_pairs={{4,0},{8,4},{12,8},{16,12},{20,16},{24,20},{28,24},{5,1},{9,5},{13... | collective-permute-start | bytes 20 | tf_op jit(solution)/shard_map/ppermute | solution.py:19
  169.4 6.3 collective-permute-start.5
  228.4 322.9 %all-reduce.7.cloned.1.call-start = ((), (), s32[]{:S(2)}) async-start(), calls=%async_computation | async-start | bytes 311296 | tf_op jit(solution)/shard_map/psum | solution.py:159
  233.5 68.6 %copy-start.11 = (f32[2,76,304]{2,0,1:T(2,128)S(1)}, f32[2,76,304]{2,0,1:T(2,128)}, u32[]{:S(2)}) copy-start(f32[2,76,304]{2,0,1:T(2,128)} %param.37) | copy-start | bytes 554500
  302.1 8.2 %copy-start = (f32[2,76,304]{2,0,1:T(2,128)S(1)}, f32[2,76,304]{2,0,1:T(2,128)}, u32[]{:S(2)}) copy-start(f32[2,76,304]{2,0,1:T(2,128)} %param.39) | copy-start | bytes 554500
  302.1 8.2 %copy-start.13 = (f32[160,2,76]{0,1,2:T(2,128)S(1)}, f32[160,2,76]{0,1,2:T(2,128)}, u32[]{:S(2)}) copy-start(f32[160,2,76]{0,1,2:T(2,128)} %get-tuple-element.104) | copy-start | bytes 291844
  386.7 12.3 %copy-start.2 = (f32[4096,76]{0,1:T(8,128)S(1)}, f32[4096,76]{0,1:T(8,128)}, u32[]{:S(2)}) copy-start(f32[4096,76]{0,1:T(8,128)} %copy-done.1) | copy-start | bytes 3735556
  441.5 4.0 collective-permute-start.6
  446.7 5.8 collective-permute-start.7
  476.4 74.9 %copy-start.12 = (f32[2,76,304]{2,0,1:T(2,128)S(1)}, f32[2,76,304]{2,0,1:T(2,128)}, u32[]{:S(2)}) copy-start(f32[2,76,304]{2,0,1:T(2,128)} %param.37) | copy-start | bytes 554500
  567.7 0.8 copy-start.4
  568.5 59.1 %copy-start.6 = (f32[2,76,304]{2,0,1:T(2,128)S(1)}, f32[2,76,304]{2,0,1:T(2,128)}, u32[]{:S(2)}) copy-start(f32[2,76,304]{2,0,1:T(2,128)} %param.38) | copy-start | bytes 554500
Sparse Core Ops, SparseCore 0:
  228.5 73.4 all-reduce.8
  480.6 70.6 all-reduce.6
where the time goes:
time: 643 us; the launch traced here: 636 us
  matrix products  173 us (27%)
  other arithmetic  132 us (21%)
  waiting for transfers between devices  129 us (20%)
  local copies, waits for them, and re-layouts  103 us (16%)
  blocking collectives  48.2 us (7%)
  between operations  29.1 us (5%)
  starting transfers between devices  21.3 us (3%)
    psum x2, waiting for transfers between devices, summed(): return lifted(lax.psum(node_part(vector, observed), 'tm'))  122 us
    dot_general x2, matrix products, precondition(): jnp.einsum('jbi,bj->bi', shaped, flat.reshape(block_count, DB), precision...  98.4 us
    scatter-add x3, other arithmetic, center_rows(): jax.ops.segment_sum(weight * values, offset, num_segments=row_count)  86.4 us
    gather x3, local copies, waits for them, and re-layouts, center_rows(): return weight * (values - jnp.take(value_sums / weight_sums, offset))  69.3 us
    dot_general x3, matrix products, node_part(): jnp.einsum('mkn,cmn->kcm', legendre.astype(jnp.float32), vector, precisio...  37.3 us
    scatter-add x1, other arithmetic, shards(): weight_sums = jax.ops.segment_sum(weight, offset, num_segments=row_count)  29 us
    dot_general x3, matrix products, lifted(): jnp.einsum('mkn,kcm->cmn', legendre.astype(jnp.float32), node_terms, prec...  25 us
    psum x2, blocking collectives, node_part(): predicted = lax.psum(partial_rows, 'order')  21.3 us
  transfers between devices with their start and end apart: 10, of which 5 were waited for; matrix products, arithmetic and copies ran while one was open for 19% of the time, Pallas kernels for 0%

commit v1 on v0

v1 whole, which is shorter than its diff:
```python
import functools

import jax
import jax.numpy as jnp
from jax import lax
from jax.experimental import pallas as pl
from jax.experimental.pallas import tpu as pltpu
from jax.sharding import PartitionSpec as P

LMAX = 300
DB = 19
SUB = 8
F32 = jnp.float32
BF16 = jnp.bfloat16
NT = (((1,), (1,)), ((), ()))
NN = (((1,), (0,)), ((), ()))
VMEM = pl.BlockSpec(memory_space=pltpu.VMEM)
ANY = pl.BlockSpec(memory_space=pl.ANY)
LIMIT = 60 * 1024 * 1024


def mm(a, b, dims=NN):
    return lax.dot_general(a, b, dims, preferred_element_type=F32)


def split2(x):
    hi = x.astype(BF16)
    return hi, (x - hi.astype(F32)).astype(BF16)


def split3(x):
    hi = x.astype(BF16)
    rest = x - hi.astype(F32)
    mid = rest.astype(BF16)
    return hi, mid, (rest - mid.astype(F32)).astype(BF16)


def pad_to(x, rows):
    if x.shape[0] == rows:
        return x
    return jnp.concatenate([x, jnp.zeros((rows - x.shape[0],) + x.shape[1:], x.dtype)], axis=0)


def sincos(angle):
    quadrant = jnp.floor(angle * 0.6366197723675814 + 0.5)
    r = angle - quadrant * 1.5703125
    r = r - quadrant * 4.8351287841796875e-4
    r = r - quadrant * 3.1385570764541626e-7
    r = r - quadrant * 6.077100506506192e-11
    q = quadrant.astype(jnp.int32)
    z = r * r
    s = ((-1.9515295891e-4 * z + 8.3321608736e-3) * z - 1.6666654611e-1) * z * r + r
    c = ((2.443315711809948e-5 * z - 1.388731625493765e-3) * z + 4.166664568298827e-2) * z * z
    c = c - 0.5 * z + 1.0
    swap = (q & 1) == 1
    cos = jnp.where(swap, s, c)
    sin = jnp.where(swap, c, s)
    cos = jnp.where(((q + 1) & 2) == 2, -cos, cos)
    sin = jnp.where((q & 2) == 2, -sin, sin)
    return cos, sin


def one_hot(count, ids):
    rows = lax.broadcasted_iota(jnp.int32, (count, ids.shape[1]), 0)
    return jnp.where(rows == ids, 1.0, 0.0).astype(BF16)


def mask_of(order, part, degrees):
    n = lax.broadcasted_iota(jnp.int32, (order.shape[0], degrees), 1)
    keep = (n <= LMAX) & (n >= jnp.maximum(order, 2))
    if part == 1:
        keep = keep & (order >= 1)
    return keep


def chunks_of(rows):
    size = 512 if rows % 512 == 0 else rows
    return [(i, size) for i in range(0, rows, size)]


def leg_copies(leg_hbm, leg, sems):
    slots = leg.shape[0]
    out = []
    for g in range(-(-slots // SUB)):
        part = pl.ds(g * SUB, min(SUB, slots - g * SUB))
        out.append(pltpu.make_async_copy(leg_hbm.at[part], leg.at[part], sems.at[g]))
    return out


def order_group(leg, copies, g, x, dims):
    if copies is not None:
        copies[g].wait()
    hi, lo = split2(x)
    x2 = jnp.concatenate([hi, lo], axis=0)
    sub = lax.broadcasted_iota(jnp.int32, x2.shape, 0) % SUB
    total = None
    for i in range(min(SUB, leg.shape[0] - g * SUB)):
        term = mm(jnp.where(sub == i, x2, jnp.zeros_like(x2)), leg[g * SUB + i], dims)
        total = term if total is None else total + term
    return total[: x.shape[0]] + total[x.shape[0] :]


def nodal_of(leg, copies, vectors, nodal_ref, pad):
    groups = -(-leg.shape[0] // SUB)
    for g in range(groups):
        x = jnp.concatenate([f(g) for v in vectors for f in v], axis=0)
        y = order_group(leg, copies, g, x, NT)
        for v in range(len(vectors)):
            for c in range(2):
                at = (2 * v + c) * SUB
                row = v * 2 * pad + c * pad + g * SUB
                nodal_ref[row : row + SUB, :] = y[at : at + SUB]


def rows_of(nodal_ref, phase_ref, node_ref, out_ref, count):
    nodes = nodal_ref.shape[1]
    wide = nodal_ref.shape[0] // count
    hi, lo = split2(nodal_ref[...])
    for at, size in chunks_of(node_ref.shape[1]):
        sel = one_hot(nodes, node_ref[:, at : at + size])
        terms = mm(hi, sel) + mm(lo, sel)
        ph = phase_ref[:, at : at + size]
        for v in range(count):
            part = terms[v * wide : (v + 1) * wide] * ph
            out_ref[v : v + 1, at : at + size] = jnp.sum(part, axis=0, keepdims=True)


def gather_nodes(u_list, phase_ref, node_ref, nodes):
    totals = [None] * len(u_list)
    for at, size in chunks_of(node_ref.shape[1]):
        sel = one_hot(nodes, node_ref[:, at : at + size])
        ph = phase_ref[:, at : at + size]
        for v, u in enumerate(u_list):
            hi, lo = split2(ph * u[:, at : at + size])
            term = mm(hi, sel, NT) + mm(lo, sel, NT)
            totals[v] = term if totals[v] is None else totals[v] + term
    return totals


def phase_kernel(lon_ref, node_ref, weight_ref, seg_ref, order_ref, phase_ref, edge_ref):
    rows = lon_ref.shape[1]
    pad = order_ref.shape[0]
    nodes = edge_ref.shape[2]
    order = order_ref[...].astype(F32)
    for at, size in chunks_of(rows):
        cos, sin = sincos(lon_ref[:, at : at + size] * order)
        phase_ref[0:pad, at : at + size] = cos
        phase_ref[pad : 2 * pad, at : at + size] = sin
    seg = seg_ref[...]
    first = jnp.min(seg, axis=1, keepdims=True)
    last = jnp.max(seg, axis=1, keepdims=True)
    w = weight_ref[...]
    parts = [jnp.where(seg == last, w, 0.0), jnp.where(seg == first, w, 0.0)]
    totals = gather_nodes(parts, phase_ref, node_ref, nodes)
    column = lax.broadcasted_iota(jnp.int32, (SUB, nodes), 1)
    for e, (ident, part) in enumerate(zip((last, first), parts)):
        edge_ref[e, 0 : 2 * pad, :] = totals[e]
        amount = jnp.sum(part, axis=1, keepdims=True)
        stats = jnp.where(column == 0, amount, ident.astype(F32) + 1.0)
        edge_ref[e, 2 * pad :, :] = stats


def forward_kernel(phase_ref, node_ref, order_ref, x_ref, d_ref, leg_hbm, out_ref, leg, nodal, sems):
    copies = leg_copies(leg_hbm, leg, sems)
    for copy in copies:
        copy.start()
    pad = order_ref.shape[0]
    slots, degrees = x_ref.shape[1], x_ref.shape[2]

    def reader(ref, c):
        def read(g):
            top = min(SUB, slots - g * SUB)
            value = ref[c, g * SUB : g * SUB + top, :]
            keep = mask_of(order_ref[g * SUB : g * SUB + top, :], c, degrees)
            return pad_to(jnp.where(keep, value, 0.0), SUB)

        return read

    vectors = [[reader(ref, c) for c in range(2)] for ref in (x_ref, d_ref)]
    nodal_of(leg, copies, vectors, nodal, pad)
    rows_of(nodal, phase_ref, node_ref, out_ref, 2)


def centered(e_list, weight, seg, prev_row, next_row, segments):
    rows = seg.shape[1]
    ids = lax.broadcasted_iota(jnp.int32, (segments, rows), 0)
    sel = jnp.where(ids == seg, 1.0, 0.0).astype(BF16)
    stack = [weight] + [weight * e for e in e_list]
    pieces = [p for s in stack for p in split3(s)]
    fill = -len(pieces) % 16
    pieces = pieces + [jnp.zeros((fill, rows), BF16)] * (fill > 0)
    sums = mm(jnp.concatenate(pieces, axis=0), sel, NT)
    sums = [sums[3 * i : 3 * i + 1] + sums[3 * i + 1 : 3 * i + 2] + sums[3 * i + 2 : 3 * i + 3] for i in range(len(stack))]
    first = jnp.min(seg, axis=1, keepdims=True)
    last = jnp.max(seg, axis=1, keepdims=True)
    lane = lax.broadcasted_iota(jnp.int32, (1, segments), 1)
    at_first, at_last = lane == first, lane == last
    join_prev = jnp.where(prev_row[:, 1:2] == first.astype(F32) + 1.0, 1.0, 0.0)
    join_next = jnp.where(next_row[:, 1:2] == last.astype(F32) + 1.0, 1.0, 0.0)
    whole = sums[0]
    whole = whole + jnp.where(at_first, join_prev * prev_row[:, 0:1], 0.0)
    whole = whole + jnp.where(at_last, join_next * next_row[:, 0:1], 0.0)
    whole = jnp.where(whole > 0.0, whole, 1.0)
    means = [s / whole for s in sums[1:]]
    pieces = [p for m in means for p in split3(m)]
    fill = -len(pieces) % 16
    pieces = pieces + [jnp.zeros((fill, segments), BF16)]
    spread = mm(jnp.concatenate(pieces, axis=0), sel)
    out = []
    for i, m in enumerate(means):
        mean = spread[3 * i : 3 * i + 1] + spread[3 * i + 1 : 3 * i + 2] + spread[3 * i + 2 : 3 * i + 3]
        to_prev = join_prev * jnp.sum(jnp.where(at_first, m, 0.0), axis=1, keepdims=True)
        to_next = join_next * jnp.sum(jnp.where(at_last, m, 0.0), axis=1, keepdims=True)
        out.append((weight * (e_list[i] - mean), to_prev, to_next))
    return out


def center_and_gather(e_list, weight_ref, seg_ref, phase_ref, node_ref, prev_ref, next_ref, out_ref, segments):
    wide, nodes = out_ref.shape[1], out_ref.shape[2]
    prev_row, next_row = (r[wide : wide + 1, :] for r in (prev_ref, next_ref))
    done = centered(e_list, weight_ref[...], seg_ref[...], prev_row, next_row, segments)
    totals = gather_nodes([u for u, _, _ in done], phase_ref, node_ref, nodes)
    for v, (_, to_prev, to_next) in enumerate(done):
        out_ref[v, :, :] = totals[v] - to_prev * prev_ref[0:wide, :] - to_next * next_ref[0:wide, :]


def back_first_kernel(segments, p_ref, grad_ref, weight_ref, seg_ref, phase_ref, node_ref, prev_ref, next_ref, out_ref):
    e_list = [grad_ref[...] - p_ref[0:1, :], p_ref[1:2, :]]
    center_and_gather(e_list, weight_ref, seg_ref, phase_ref, node_ref, prev_ref, next_ref, out_ref, segments)


def scalars_of(row):
    return [row[:, i : i + 1] for i in range(4)]


def back_next_kernel(segments, p_ref, before_ref, weight_ref, seg_ref, phase_ref, node_ref, prev_ref, next_ref, out_ref):
    rows = seg_ref.shape[1]
    step, beta = steps_of(p_ref[0:1, rows : rows + 4])
    e = p_ref[0:1, 0:rows] - step * p_ref[1:2, 0:rows] - beta * before_ref[1:2, :]
    center_and_gather([e], weight_ref, seg_ref, phase_ref, node_ref, prev_ref, next_ref, out_ref, segments)


def steps_of(row):
    residual_dot, curvature, first, second = scalars_of(row)
    step = residual_dot / curvature
    return step, (first - step * second) / curvature


def lifted(leg, copies, gathered_ref, count, pad, store):
    groups = -(-leg.shape[0] // SUB)
    for g in range(groups):
        x = jnp.concatenate(
            [gathered_ref[v, c * pad + g * SUB : c * pad + (g + 1) * SUB, :] for v in range(count) for c in range(2)],
            axis=0,
        )
        y = order_group(leg, copies, g, x, NN)
        for v in range(count):
            for c in range(2):
                at = (2 * v + c) * SUB
                store(v, c, g, y[at : at + SUB])


def precondition(pre, start_row, vectors_ref, out_ref, count, pad):
    degrees = vectors_ref.shape[1]
    hi, lo = split2(vectors_ref[...])
    slots = pre.shape[2]
    source = lax.broadcasted_iota(jnp.int32, (degrees, degrees), 0) - start_row
    out_ref[...] = jnp.zeros_like(out_ref)
    for l in range(DB):
        spread = jnp.where(source == l, 1.0, 0.0).astype(BF16)
        wide = mm(hi, spread) + mm(lo, spread)
        for v in range(count):
            for c in range(2):
                at = (2 * v + c) * pad
                out_ref[at : at + slots, :] += pre[l, c] * wide[at : at + slots]


def dot_sum(pairs):
    total = None
    for a, b in pairs:
        term = jnp.sum(jnp.sum(a * b, axis=1, keepdims=True), axis=0, keepdims=True)
        total = term if total is None else total + term
    return total


def scalar_row(values, width):
    lane = lax.broadcasted_iota(jnp.int32, (1, width), 1)
    row = jnp.zeros((1, width), F32)
    for i, value in enumerate(values):
        row = jnp.where(lane == i, value, row)
    return row


def middle_kernel(
    gathered_ref, phase_ref, node_ref, order_ref, start_ref, kaula_ref, x_ref, d_ref, leg_hbm, pre_hbm,
    out_ref, r_ref, q_ref, pr_ref, pq_ref,
    leg, pre, nodal, vec, smooth, sems, pre_sem,
):
    copies = leg_copies(leg_hbm, leg, sems)
    for copy in copies:
        copy.start()
    pre_copy = pltpu.make_async_copy(pre_hbm, pre, pre_sem)
    pre_copy.start()
    pad = order_ref.shape[0]
    slots, degrees = x_ref.shape[1], x_ref.shape[2]
    rows = node_ref.shape[1]

    def store(v, c, g, y):
        at = (2 * v + c) * pad + g * SUB
        top = min(SUB, slots - g * SUB)
        part = slice(g * SUB, g * SUB + top)
        keep = mask_of(order_ref[part, :], c, degrees)
        k = kaula_ref[c, part, :]
        value = y[:top] - k * x_ref[c, part, :] if v == 0 else y[:top] + k * d_ref[c, part, :]
        vec[at : at + SUB, :] = pad_to(jnp.where(keep, value, 0.0), SUB)

    lifted(leg, copies, gathered_ref, 2, pad, store)
    pre_copy.wait()
    precondition(pre, start_ref[...], vec, smooth, 2, pad)
    dots = [[], [], [], []]
    for c in range(2):
        keep = mask_of(order_ref[0:slots, :], c, degrees)
        a, b = c * pad, (2 + c) * pad
        r, q = vec[a : a + slots, :], vec[b : b + slots, :]
        pr = jnp.where(keep, smooth[a : a + slots, :], 0.0)
        pq = jnp.where(keep, smooth[b : b + slots, :], 0.0)
        d = jnp.where(keep, d_ref[c], 0.0)
        smooth[a : a + slots, :] = pr
        smooth[b : b + slots, :] = pq
        r_ref[c], q_ref[c], pr_ref[c], pq_ref[c] = r, q, pr, pq
        for i, pair in enumerate(((r, d), (d, q), (pr, q), (pq, q))):
            dots[i].append(pair)
    out_ref[0:1, rows:] = scalar_row([dot_sum(p) for p in dots], out_ref.shape[1] - rows)
    out_ref[1:2, rows:] = jnp.zeros((1, out_ref.shape[1] - rows), F32)

    def reader(v, c):
        return lambda g: smooth[(2 * v + c) * pad + g * SUB : (2 * v + c) * pad + (g + 1) * SUB, :]

    nodal_of(leg, None, [[reader(v, c) for c in range(2)] for v in range(2)], nodal, pad)
    rows_of(nodal, phase_ref, node_ref, out_ref, 2)


def last_kernel(
    gathered_ref, row_ref, order_ref, start_ref, kaula_ref, x_ref, d_ref, r_ref, q_ref, pr_ref, pq_ref, leg_hbm, pre_hbm,
    dots_ref, q1_ref, pq1_ref, x1_ref, d1_ref, r1_ref, pr1_ref,
    leg, pre, vec, smooth, sems, pre_sem,
):
    copies = leg_copies(leg_hbm, leg, sems)
    for copy in copies:
        copy.start()
    pre_copy = pltpu.make_async_copy(pre_hbm, pre, pre_sem)
    pre_copy.start()
    pad = order_ref.shape[0]
    slots, degrees = x_ref.shape[1], x_ref.shape[2]
    step, beta = steps_of(row_ref[0:1, 0:4])
    for c in range(2):
        keep = mask_of(order_ref[0:slots, :], c, degrees)
        d = jnp.where(keep, d_ref[c], 0.0)
        pr1 = pr_ref[c] - step * pq_ref[c]
        x1_ref[c] = jnp.where(keep, x_ref[c], 0.0) + step * d
        r1_ref[c] = r_ref[c] - step * q_ref[c]
        pr1_ref[c] = pr1
        d1_ref[c] = pr1 - beta * d

    def store(v, c, g, y):
        at = c * pad + g * SUB
        top = min(SUB, slots - g * SUB)
        part = slice(g * SUB, g * SUB + top)
        keep = mask_of(order_ref[part, :], c, degrees)
        value = y[:top] + kaula_ref[c, part, :] * d1_ref[c, part, :]
        vec[at : at + SUB, :] = pad_to(jnp.where(keep, value, 0.0), SUB)

    lifted(leg, copies, gathered_ref, 1, pad, store)
    pre_copy.wait()
    precondition(pre, start_ref[...], vec, smooth, 1, pad)
    dots = [[], [], [], []]
    for c in range(2):
        keep = mask_of(order_ref[0:slots, :], c, degrees)
        q = vec[c * pad : c * pad + slots, :]
        pq = jnp.where(keep, smooth[c * pad : c * pad + slots, :], 0.0)
        q1_ref[c], pq1_ref[c] = q, pq
        d = d1_ref[c]
        for i, pair in enumerate(((r1_ref[c], d), (d, q), (pr1_ref[c], q), (pq, q))):
            dots[i].append(pair)
    dots_ref[...] = scalar_row([dot_sum(p) for p in dots], dots_ref.shape[1])


def butterfly(x, axis):
    size = lax.axis_size(axis)
    step = 1
    while step < size:
        x = x + lax.ppermute(x, axis, [(i, i ^ step) for i in range(size)])
        step *= 2
    return x


def call(kernel, outs, scratch, n_in, any_in=()):
    specs = [ANY if i in any_in else VMEM for i in range(n_in)]
    return pl.pallas_call(
        kernel,
        out_shape=[jax.ShapeDtypeStruct(s, F32) for s in outs],
        in_specs=specs,
        out_specs=[VMEM for _ in outs],
        scratch_shapes=scratch,
        compiler_params=pltpu.CompilerParams(vmem_limit_bytes=LIMIT),
    )


def shards(longitude, node_index, weight, gradient, segment, order_map, legendre, precond, kaula, start, direction):
    rows = longitude.shape[0]
    slots, nodes, degrees = legendre.shape
    pad = -(-slots // SUB) * SUB
    wide = 2 * pad
    segments = lax.axis_size("tm") * lax.axis_size("order")
    line = lambda v: v.reshape(1, rows)
    lon, node, w, grad, seg = (line(v) for v in (longitude, node_index, weight, gradient, segment))
    order = pad_to(order_map, pad).reshape(pad, 1)
    starts = ((jnp.arange(degrees, dtype=jnp.int32) // DB) * DB).reshape(1, degrees)
    coef = (2, slots, degrees)
    groups = -(-slots // SUB)
    leg_scratch = [pltpu.VMEM(legendre.shape, BF16)]
    leg_sems = pltpu.SemaphoreType.DMA((groups,))

    phase, edges = call(phase_kernel, [(wide, rows), (2, wide + SUB, nodes)], [], 5)(lon, node, w, seg, order)
    size = lax.axis_size("tm")
    up = [(i, i + 1) for i in range(size - 1)]
    prev_edge = lax.ppermute(edges[0], "tm", up)
    next_edge = lax.ppermute(edges[1], "tm", [(b, a) for a, b in up])

    (part,) = call(
        forward_kernel, [(2, rows)], leg_scratch + [pltpu.VMEM((2 * wide, nodes), F32), leg_sems], 6, (5,)
    )(phase, node, order, start, direction, legendre)
    first_rows = butterfly(part, "order")
    (part,) = call(functools.partial(back_first_kernel, segments), [(2, wide, nodes)], [], 8)(
        first_rows, grad, w, seg, phase, node, prev_edge, next_edge
    )
    gathered = butterfly(part, "tm")
    coef_scratch = leg_scratch + [pltpu.VMEM(precond.shape, F32)]
    part, r0, q0, pr0, pq0 = call(
        middle_kernel,
        [(2, rows + 128)] + [coef] * 4,
        coef_scratch
        + [pltpu.VMEM((2 * wide, nodes), F32)]
        + [pltpu.VMEM((2 * wide, degrees), F32)] * 2
        + [leg_sems, pltpu.SemaphoreType.DMA(())],
        10,
        (8, 9),
    )(gathered, phase, node, order, starts, kaula, start, direction, legendre, precond)
    next_rows = butterfly(part, "order")
    (part,) = call(functools.partial(back_next_kernel, segments), [(1, wide, nodes)], [], 8)(
        next_rows, first_rows, w, seg, phase, node, prev_edge, next_edge
    )
    gathered = butterfly(part, "tm")
    row = lax.slice(next_rows, (0, rows), (1, rows + 128))
    dots, q1, pq1, x1, d1, r1, pr1 = call(
        last_kernel,
        [(1, 128)] + [coef] * 6,
        coef_scratch + [pltpu.VMEM((wide, degrees), F32)] * 2 + [leg_sems, pltpu.SemaphoreType.DMA(())],
        13,
        (11, 12),
    )(gathered, row, order, starts, kaula, start, direction, r0, q0, pr0, pq0, legendre, precond)
    dots = butterfly(dots, "order")
    step, beta = (s[0, 0] for s in steps_of(dots))
    return x1 + step * d1, r1 - step * q1, pr1 - step * pq1 - beta * d1


def solution(mesh):
    coef = P(None, "order", None)
    placed = (P("tm"),) * 5 + (P("order"), P("order", None, None), P(None, None, "order", None), coef, coef, coef)
    return jax.shard_map(shards, mesh=mesh, in_specs=placed, out_specs=(coef, coef, coef), check_vma=False)
```

time: 643 us -> 157 us (0.24)
  matrix products: 173 us -> 0 us
  other arithmetic: 132 us -> 9.02 us
  local copies, waits for them, and re-layouts: 103 us -> 16.3 us
  waiting for transfers between devices: 129 us -> 45.1 us
  Pallas kernels: 0 us -> 59.6 us
  blocking collectives: 48.2 us -> 0 us
  between operations: 29.1 us -> 4.06 us
    dot_general x14 -> x0, matrix products: 173 us -> none  [the longest x2 98.4 us: precondition(): jnp.einsum('jbi,bj->bi', shaped, flat.reshape(block_count, DB), precision...]
    psum x2 -> x0, waiting for transfers between devices: 122 us -> none  [summed(): return lifted(lax.psum(node_part(vector, observed), 'tm'))]
    scatter-add x9 -> x0, other arithmetic: 116 us -> none  [the longest x3 86.4 us: center_rows(): jax.ops.segment_sum(weight * values, offset, num_segments=row_count)]
    gather x3 -> x0, local copies, waits for them, and re-layouts: 69.3 us -> none  [center_rows(): return weight * (values - jnp.take(value_sums / weight_sums, offset))]
    pallas_call x0 -> x6, Pallas kernels: none -> 59.6 us  [the longest x1 20.1 us: shards(): call(middle_kernel, [(2, rows + 128)] + [coef] * 4, coef_scratch + [pltpu...]
    psum x6 -> x0, blocking collectives: 48.2 us -> none  [the longest x2 21.3 us: node_part(): predicted = lax.psum(partial_rows, 'order')]
    ppermute x8 -> x14, waiting for transfers between devices: 7.07 us -> 45.1 us  [the longest x12 45.1 us: butterfly(): x = x + lax.ppermute(x, axis, [(i, i ^ step) for i in range(size)])]
    reshape x12 -> x2, local copies, waits for them, and re-layouts: 21.9 us -> 1.38 us  [shards(): order = pad_to(order_map, pad).reshape(pad, 1)]
  transfers between devices with their start and end apart: 10 -> 14, of which waited for: 5 -> 12; matrix products, arithmetic and copies ran while one was open for 19% -> 8% of each run, Pallas kernels for 0% -> 9%
where the time goes in v1:
time: 157 us; the launch traced here: 156 us
  Pallas kernels  59.6 us (38%)
  waiting for transfers between devices  45.1 us (29%)
  starting transfers between devices  22 us (14%)
  local copies, waits for them, and re-layouts  16.3 us (10%)
  other arithmetic  9.02 us (6%)
  between operations  4.06 us (3%)
    ppermute x12, waiting for transfers between devices, butterfly(): x = x + lax.ppermute(x, axis, [(i, i ^ step) for i in range(size)])  45.1 us
    pallas_call x1, Pallas kernels, shards(): call(middle_kernel, [(2, rows + 128)] + [coef] * 4, coef_scratch + [pltpu...  20.1 us
    ppermute x12, starting transfers between devices, butterfly(): x = x + lax.ppermute(x, axis, [(i, i ^ step) for i in range(size)])  15 us
    pallas_call x1, Pallas kernels, shards(): call(forward_kernel, [(2, rows)], leg_scratch + [pltpu.VMEM((2 * wide, no...  13.6 us
    unnamed x13, local copies, waits for them, and re-layouts  12.1 us
    pallas_call x1, Pallas kernels, shards(): call(last_kernel, [(1, 128)] + [coef] * 6, coef_scratch + [pltpu.VMEM((wi...  11 us
    add x12, other arithmetic, butterfly(): x = x + lax.ppermute(x, axis, [(i, i ^ step) for i in range(size)])  6.93 us
    pallas_call x1, Pallas kernels, shards(): call(phase_kernel, [(wide, rows), (2, wide + SUB, nodes)], [], 5)  5.84 us
  transfers between devices with their start and end apart: 14, of which 12 were waited for; matrix products, arithmetic and copies ran while one was open for 8% of the time, Pallas kernels for 9%

profile of v1, /device:TPU:0, one launch (start us, length us, event | category | flops | bytes accessed | tf_op | source)
XLA Modules:
  0.0 156.2 jit_solution(13913049899886727681)
XLA Ops:
  2.0 5.8 %shard_map.130 = (f32[160,4096]{1,0:T(8,128)}, f32[2,168,160]{2,1,0:T(8,128)}) custom-call(f32[1,4096]{1,0:T(1,128)} %bitcast.25, s32[1,4096]{1,0:T(1,128)} %bitcast.13, f32[1,4096]{1,0:T(1,128)} %bitcast.18, s32[1,4096]{1,0:T(1,128)} %bitcast.21, s32[80,1]{1,0:T(8,128)} %copy.14.order_ref), custom_call_target="tpu_custom_call" | custom-call | tf_op jit(solution)/shard_map/pallas_call | solution.py:424
  8.9 1.3 collective-permute-start.3
  10.2 5.7 %collective-permute-start.2 = (f32[168,160]{1,0:T(8,128)S(1)}, f32[168,160]{1,0:T(8,128)S(1)}, u32[]{:S(2)}, u32[]{:S(2)}) collective-permute-start(f32[168,160]{1,0:T(8,128)S(1)} %get-tuple-element.35), channel_id=1, source_target_pairs={{0,4},{4,8},{8,12},{12,16},{16,20},{20,24},{24,28},{1,5},{5,9},{9,... | collective-permute-start | bytes 322568 | tf_op jit(solution)/shard_map/ppermute | solution.py:427
  15.9 1.7 %copy.16.x_ref = f32[2,76,304]{2,1,0:T(8,128)} copy(f32[2,76,304]{2,0,1:T(2,128)} %param.20) | data formatting | bytes 369664 | tf_op args[9]
  17.6 1.7 %copy.17.d_ref = f32[2,76,304]{2,1,0:T(8,128)} copy(f32[2,76,304]{2,0,1:T(2,128)} %param.21) | data formatting | bytes 369664 | tf_op args[10]
  19.3 13.6 %shard_map.131 = f32[2,4096]{1,0:T(2,128)} custom-call(f32[160,4096]{1,0:T(8,128)} %get-tuple-element.17.phase_ref, s32[1,4096]{1,0:T(1,128)} %bitcast.14, s32[80,1]{1,0:T(8,128)} %copy.14.order_ref, f32[2,76,304]{2,1,0:T(8,128)} %copy.16.x_ref, f32[2,76,304]{2,1,0:T(8,128)} %copy.17.d_ref, bf16[76,160,304]{2,1,0:T(8,128)(2,1)} %leg_hbm.5), custom_call_target="tpu_custom_call" | custom-call | tf_op jit(solution)/shard_map/pallas_call | solution.py:430
  33.0 1.4 collective-permute-done
  35.2 2.1 %collective-permute-start.1 = (f32[2,4096]{1,0:T(2,128)S(1)}, f32[2,4096]{1,0:T(2,128)S(1)}, u32[]{:S(2)}, u32[]{:S(2)}) collective-permute-start(f32[2,4096]{1,0:T(2,128)S(1)} %add.49), channel_id=1, source_target_pairs={{0,2},{1,3},{2,0},{3,1},{4,6},{5,7},{6,4},{7,5},{8,10},{9,11},{10,... | collective-permute-start | bytes 98312 | tf_op jit(solution)/shard_map/ppermute | solution.py:392
  37.2 1.9 %collective-permute-done.1 = f32[2,4096]{1,0:T(2,128)S(1)} collective-permute-done((f32[2,4096]{1,0:T(2,128)S(1)}, f32[2,4096]{1,0:T(2,128)S(1)}, u32[]{:S(2)}, u32[]{:S(2)}) %collective-permute-start.1) | collective-permute-done | bytes 32800 | tf_op jit(solution)/shard_map/ppermute | solution.py:392
  40.5 4.8 %shard_map.132 = f32[2,160,160]{2,1,0:T(8,128)} custom-call(f32[2,4096]{1,0:T(2,128)} %add.50.p_ref.before_ref, f32[1,4096]{1,0:T(1,128)} %bitcast.24, f32[1,4096]{1,0:T(1,128)} %bitcast.19, s32[1,4096]{1,0:T(1,128)} %bitcast.22, f32[160,4096]{1,0:T(8,128)} %get-tuple-element.17.phase_ref, s32[1,4096]{1,0:T(1,128)} %bitcast.15, f32[168,160]{1,0:T(8,128)} %copy-done.1, ...), custom_call_target="tpu_custom_call" | custom-call | tf_op jit(solution)/shard_map/pallas_call | solution.py:434
  45.3 2.9 %collective-permute-start.4 = (f32[2,160,160]{2,1,0:T(8,128)}, f32[2,160,160]{2,1,0:T(8,128)S(1)}, u32[]{:S(2)}, u32[]{:S(2)}) collective-permute-start(f32[2,160,160]{2,1,0:T(8,128)} %shard_map.132), channel_id=1, source_target_pairs={{0,4},{4,0},{8,12},{12,8},{16,20},{20,16},{24,28},{28,24},{1,5},{5... | collective-permute-start | bytes 614408 | tf_op jit(solution)/shard_map/ppermute | solution.py:392
  48.2 7.1 %collective-permute-done.4 = f32[2,160,160]{2,1,0:T(8,128)S(1)} collective-permute-done((f32[2,160,160]{2,1,0:T(8,128)}, f32[2,160,160]{2,1,0:T(8,128)S(1)}, u32[]{:S(2)}, u32[]{:S(2)}) %collective-permute-start.4) | collective-permute-done | bytes 204832 | tf_op jit(solution)/shard_map/ppermute | solution.py:392
  56.3 1.6 %collective-permute-start.5 = (f32[2,160,160]{2,1,0:T(8,128)S(1)}, f32[2,160,160]{2,1,0:T(8,128)S(1)}, u32[]{:S(2)}, u32[]{:S(2)}) collective-permute-start(f32[2,160,160]{2,1,0:T(8,128)S(1)} %add.51), channel_id=1, source_target_pairs={{0,8},{4,12},{8,0},{12,4},{16,24},{20,28},{24,16},{28,20},{1,9},{5... | collective-permute-start | bytes 614408 | tf_op jit(solution)/shard_map/ppermute | solution.py:392
  58.0 6.5 %collective-permute-done.5 = f32[2,160,160]{2,1,0:T(8,128)S(1)} collective-permute-done((f32[2,160,160]{2,1,0:T(8,128)S(1)}, f32[2,160,160]{2,1,0:T(8,128)S(1)}, u32[]{:S(2)}, u32[]{:S(2)}) %collective-permute-start.5) | collective-permute-done | bytes 204832 | tf_op jit(solution)/shard_map/ppermute | solution.py:392
  64.5 2.6 %collective-permute-start.6 = (f32[2,160,160]{2,1,0:T(8,128)S(1)}, f32[2,160,160]{2,1,0:T(8,128)S(1)}, u32[]{:S(2)}, u32[]{:S(2)}) collective-permute-start(f32[2,160,160]{2,1,0:T(8,128)S(1)} %add.52), channel_id=1, source_target_pairs={{0,16},{4,20},{8,24},{12,28},{16,0},{20,4},{24,8},{28,12},{1,17},{... | collective-permute-start | bytes 614408 | tf_op jit(solution)/shard_map/ppermute | solution.py:392
  67.9 4.9 %copy.22.pre_hbm = f32[19,2,76,304]{3,2,1,0:T(8,128)} copy(f32[19,2,76,304]{3,1,2,0:T(2,128)} %param.18) | data formatting | bytes 7023616 | tf_op args[7]
  73.3 6.4 %collective-permute-done.6 = f32[2,160,160]{2,1,0:T(8,128)S(1)} collective-permute-done((f32[2,160,160]{2,1,0:T(8,128)S(1)}, f32[2,160,160]{2,1,0:T(8,128)S(1)}, u32[]{:S(2)}, u32[]{:S(2)}) %collective-permute-start.6) | collective-permute-done | bytes 204832 | tf_op jit(solution)/shard_map/ppermute | solution.py:392
  80.4 20.1 %shard_map.133 = (f32[2,4224]{1,0:T(2,128)}, f32[2,76,304]{2,1,0:T(8,128)}, f32[2,76,304]{2,1,0:T(8,128)}, f32[2,76,304]{2,1,0:T(8,128)}, f32[2,76,304]{2,1,0:T(8,128)}) custom-call(f32[2,160,160]{2,1,0:T(8,128)} %add.53.gathered_ref, f32[160,4096]{1,0:T(8,128)} %get-tuple-element.17.phase_ref, s32[1,4096]{1,0:T(1,128)} %bitcast.16, ...), custom_call_target="tpu_custom_call" | custom-call | tf_op jit(solution)/shard_map/pallas_call | solution.py:439
  100.7 1.4 collective-permute-done.7
  102.9 1.6 collective-permute-start.8
  104.4 2.4 %collective-permute-done.8 = f32[2,4224]{1,0:T(2,128)S(1)} collective-permute-done((f32[2,4224]{1,0:T(2,128)S(1)}, f32[2,4224]{1,0:T(2,128)S(1)}, u32[]{:S(2)}, u32[]{:S(2)}) %collective-permute-start.8) | collective-permute-done | bytes 33824 | tf_op jit(solution)/shard_map/ppermute | solution.py:392
  107.5 4.2 %shard_map.134 = f32[1,160,160]{2,1,0:T(8,128)} custom-call(f32[2,4224]{1,0:T(2,128)} %add.55.p_ref, f32[2,4096]{1,0:T(2,128)} %add.50.p_ref.before_ref, f32[1,4096]{1,0:T(1,128)} %bitcast.20, s32[1,4096]{1,0:T(1,128)} %bitcast.23, f32[160,4096]{1,0:T(8,128)} %get-tuple-element.17.phase_ref, s32[1,4096]{1,0:T(1,128)} %bitcast.17, f32[168,160]{1,0:T(8,128)} %copy-done.1, ...), custom_call_target="tpu_custom_call" | custom-call | tf_op jit(solution)/shard_map/pallas_call | solution.py:450
  111.7 1.2 collective-permute-start.9
  112.8 4.3 %collective-permute-done.9 = f32[1,160,160]{2,1,0:T(8,128)S(1)} collective-permute-done((f32[1,160,160]{2,1,0:T(8,128)}, f32[1,160,160]{2,1,0:T(8,128)S(1)}, u32[]{:S(2)}, u32[]{:S(2)}) %collective-permute-start.9) | collective-permute-done | bytes 102432 | tf_op jit(solution)/shard_map/ppermute | solution.py:392
  118.2 5.3 %collective-permute-done.10 = f32[1,160,160]{2,1,0:T(8,128)S(1)} collective-permute-done((f32[1,160,160]{2,1,0:T(8,128)S(1)}, f32[1,160,160]{2,1,0:T(8,128)S(1)}, u32[]{:S(2)}, u32[]{:S(2)}) %collective-permute-start.10) | collective-permute-done | bytes 102432 | tf_op jit(solution)/shard_map/ppermute | solution.py:392
  123.5 1.3 collective-permute-start.11
  126.0 5.0 %collective-permute-done.11 = f32[1,160,160]{2,1,0:T(8,128)S(1)} collective-permute-done((f32[1,160,160]{2,1,0:T(8,128)S(1)}, f32[1,160,160]{2,1,0:T(8,128)S(1)}, u32[]{:S(2)}, u32[]{:S(2)}) %collective-permute-start.11) | collective-permute-done | bytes 102432 | tf_op jit(solution)/shard_map/ppermute | solution.py:392
  131.7 11.0 %shard_map.135 = (f32[1,128]{1,0:T(1,128)}, f32[2,76,304]{2,1,0:T(8,128)}, f32[2,76,304]{2,1,0:T(8,128)}, f32[2,76,304]{2,1,0:T(8,128)}, f32[2,76,304]{2,1,0:T(8...) custom-call(f32[1,160,160]{2,1,0:T(8,128)} %add.58.gathered_ref, f32[1,128]{1,0:T(1,128)} %slice.28.row_ref, ...), custom_call_target="tpu_custom_call" | custom-call | tf_op jit(solution)/shard_map/pallas_call | solution.py:455
  142.8 1.3 collective-permute-done.12
  144.8 1.5 collective-permute-start.13
  146.3 2.1 %collective-permute-done.13 = f32[1,128]{1,0:T(1,128)S(1)} collective-permute-done((f32[1,128]{1,0:T(1,128)S(1)}, f32[1,128]{1,0:T(1,128)S(1)}, u32[]{:S(2)}, u32[]{:S(2)}) %collective-permute-start.13) | collective-permute-done | bytes 544 | tf_op jit(solution)/shard_map/ppermute | solution.py:392
  152.2 1.5 multiply_subtract_fusion
  (34 shorter events, 15.8 us)
Async XLA Ops:
  8.9 30.9 %collective-permute-start.3 = (f32[168,160]{1,0:T(8,128)S(1)}, f32[168,160]{1,0:T(8,128)S(1)}, u32[]{:S(2)}, u32[]{:S(2)}) collective-permute-start(f32[168,160]{1,0:T(8,128)S(1)} %get-tuple-element.34), channel_id=1, source_target_pairs={{4,0},{8,4},{12,8},{16,12},{20,16},{24,20},{28,24},{5,1},{9,5},{13... | collective-permute-start | bytes 322568 | tf_op jit(solution)/shard_map/ppermute | solution.py:428
  10.2 29.6 %collective-permute-start.2 = (f32[168,160]{1,0:T(8,128)S(1)}, f32[168,160]{1,0:T(8,128)S(1)}, u32[]{:S(2)}, u32[]{:S(2)}) collective-permute-start(f32[168,160]{1,0:T(8,128)S(1)} %get-tuple-element.35), channel_id=1, source_target_pairs={{0,4},{4,8},{8,12},{12,16},{16,20},{20,24},{24,28},{1,5},{5,9},{9,... | collective-permute-start | bytes 322568 | tf_op jit(solution)/shard_map/ppermute | solution.py:427
  32.9 34.2 %copy-start.2 = (f32[2,76,304]{2,0,1:T(2,128)S(1)}, f32[2,76,304]{2,0,1:T(2,128)}, u32[]{:S(2)}) copy-start(f32[2,76,304]{2,0,1:T(2,128)} %param.19) | copy-start | bytes 554500
  32.9 1.5 collective-permute-start
  35.2 4.0 %collective-permute-start.1 = (f32[2,4096]{1,0:T(2,128)S(1)}, f32[2,4096]{1,0:T(2,128)S(1)}, u32[]{:S(2)}, u32[]{:S(2)}) collective-permute-start(f32[2,4096]{1,0:T(2,128)S(1)} %add.49), channel_id=1, source_target_pairs={{0,2},{1,3},{2,0},{3,1},{4,6},{5,7},{6,4},{7,5},{8,10},{9,11},{10,... | collective-permute-start | bytes 98312 | tf_op jit(solution)/shard_map/ppermute | solution.py:392
  39.8 0.7 copy-start
  39.8 0.7 copy-start.1
  45.3 10.0 %collective-permute-start.4 = (f32[2,160,160]{2,1,0:T(8,128)}, f32[2,160,160]{2,1,0:T(8,128)S(1)}, u32[]{:S(2)}, u32[]{:S(2)}) collective-permute-start(f32[2,160,160]{2,1,0:T(8,128)} %shard_map.132), channel_id=1, source_target_pairs={{0,4},{4,0},{8,12},{12,8},{16,20},{20,16},{24,28},{28,24},{1,5},{5... | collective-permute-start | bytes 614408 | tf_op jit(solution)/shard_map/ppermute | solution.py:392
  56.3 8.1 %collective-permute-start.5 = (f32[2,160,160]{2,1,0:T(8,128)S(1)}, f32[2,160,160]{2,1,0:T(8,128)S(1)}, u32[]{:S(2)}, u32[]{:S(2)}) collective-permute-start(f32[2,160,160]{2,1,0:T(8,128)S(1)} %add.51), channel_id=1, source_target_pairs={{0,8},{4,12},{8,0},{12,4},{16,24},{20,28},{24,16},{28,20},{1,9},{5... | collective-permute-start | bytes 614408 | tf_op jit(solution)/shard_map/ppermute | solution.py:392
  64.5 15.2 %collective-permute-start.6 = (f32[2,160,160]{2,1,0:T(8,128)S(1)}, f32[2,160,160]{2,1,0:T(8,128)S(1)}, u32[]{:S(2)}, u32[]{:S(2)}) collective-permute-start(f32[2,160,160]{2,1,0:T(8,128)S(1)} %add.52), channel_id=1, source_target_pairs={{0,16},{4,20},{8,24},{12,28},{16,0},{20,4},{24,8},{28,12},{1,17},{... | collective-permute-start | bytes 614408 | tf_op jit(solution)/shard_map/ppermute | solution.py:392
  100.6 1.5 collective-permute-start.7
  102.9 4.0 %collective-permute-start.8 = (f32[2,4224]{1,0:T(2,128)S(1)}, f32[2,4224]{1,0:T(2,128)S(1)}, u32[]{:S(2)}, u32[]{:S(2)}) collective-permute-start(f32[2,4224]{1,0:T(2,128)S(1)} %add.54), channel_id=1, source_target_pairs={{0,2},{1,3},{2,0},{3,1},{4,6},{5,7},{6,4},{7,5},{8,10},{9,11},{10,... | collective-permute-start | bytes 101384 | tf_op jit(solution)/shard_map/ppermute | solution.py:392
  111.7 5.5 %collective-permute-start.9 = (f32[1,160,160]{2,1,0:T(8,128)}, f32[1,160,160]{2,1,0:T(8,128)S(1)}, u32[]{:S(2)}, u32[]{:S(2)}) collective-permute-start(f32[1,160,160]{2,1,0:T(8,128)} %shard_map.134), channel_id=1, source_target_pairs={{0,4},{4,0},{8,12},{12,8},{16,20},{20,16},{24,28},{28,24},{1,5},{5... | collective-permute-start | bytes 307208 | tf_op jit(solution)/shard_map/ppermute | solution.py:392
  118.1 5.4 %collective-permute-start.10 = (f32[1,160,160]{2,1,0:T(8,128)S(1)}, f32[1,160,160]{2,1,0:T(8,128)S(1)}, u32[]{:S(2)}, u32[]{:S(2)}) collective-permute-start(f32[1,160,160]{2,1,0:T(8,128)S(1)} %add.56), channel_id=1, source_target_pairs={{0,8},{4,12},{8,0},{12,4},{16,24},{20,28},{24,16},{28,20},{1,9},{5... | collective-permute-start | bytes 307208 | tf_op jit(solution)/shard_map/ppermute | solution.py:392
  123.5 7.5 %collective-permute-start.11 = (f32[1,160,160]{2,1,0:T(8,128)S(1)}, f32[1,160,160]{2,1,0:T(8,128)S(1)}, u32[]{:S(2)}, u32[]{:S(2)}) collective-permute-start(f32[1,160,160]{2,1,0:T(8,128)S(1)} %add.57), channel_id=1, source_target_pairs={{0,16},{4,20},{8,24},{12,28},{16,0},{20,4},{24,8},{28,12},{1,17},{... | collective-permute-start | bytes 307208 | tf_op jit(solution)/shard_map/ppermute | solution.py:392
  142.7 1.4 collective-permute-start.12
  144.8 3.6 %collective-permute-start.13 = (f32[1,128]{1,0:T(1,128)S(1)}, f32[1,128]{1,0:T(1,128)S(1)}, u32[]{:S(2)}, u32[]{:S(2)}) collective-permute-start(f32[1,128]{1,0:T(1,128)S(1)} %add.59), channel_id=1, source_target_pairs={{0,2},{1,3},{2,0},{3,1},{4,6},{5,7},{6,4},{7,5},{8,10},{9,11},{10,... | collective-permute-start | bytes 1544 | tf_op jit(solution)/shard_map/ppermute | solution.py:392

commit v2 on v1

v2 whole, which is shorter than its diff:
```python
import functools

import jax
import jax.numpy as jnp
from jax import lax
from jax.experimental import pallas as pl
from jax.experimental.pallas import tpu as pltpu
from jax.sharding import PartitionSpec as P

LMAX = 300
DB = 19
SUB = 8
HALF = 4
LANES = 128
LON, NODE, WEIGHT, SEG, GRAD, ORDER = range(6)
F32 = jnp.float32
BF16 = jnp.bfloat16
NT = (((1,), (1,)), ((), ()))
NN = (((1,), (0,)), ((), ()))
VMEM = pl.BlockSpec(memory_space=pltpu.VMEM)
HBM = pl.BlockSpec(memory_space=pltpu.HBM)
LIMIT = 28 * 1024 * 1024


def mm(a, b, dims=NN):
    return lax.dot_general(a, b, dims, preferred_element_type=F32)


def split2(x):
    hi = x.astype(BF16)
    return hi, (x - hi.astype(F32)).astype(BF16)


def split3(x):
    hi = x.astype(BF16)
    rest = x - hi.astype(F32)
    mid = rest.astype(BF16)
    return hi, mid, (rest - mid.astype(F32)).astype(BF16)


def sincos(angle):
    quadrant = jnp.floor(angle * 0.6366197723675814 + 0.5)
    r = angle - quadrant * 1.5703125
    r = r - quadrant * 4.8351287841796875e-4
    r = r - quadrant * 3.1385570764541626e-7
    r = r - quadrant * 6.077100506506192e-11
    q = quadrant.astype(jnp.int32)
    z = r * r
    s = ((-1.9515295891e-4 * z + 8.3321608736e-3) * z - 1.6666654611e-1) * z * r + r
    c = ((2.443315711809948e-5 * z - 1.388731625493765e-3) * z + 4.166664568298827e-2) * z * z
    c = c - 0.5 * z + 1.0
    swap = (q & 1) == 1
    cos = jnp.where(swap, s, c)
    sin = jnp.where(swap, c, s)
    cos = jnp.where(((q + 1) & 2) == 2, -cos, cos)
    sin = jnp.where((q & 2) == 2, -sin, sin)
    return cos, sin


def one_hot(count, ids):
    rows = lax.broadcasted_iota(jnp.int32, (count, ids.shape[1]), 0)
    return jnp.where(rows == ids, 1.0, 0.0).astype(BF16)


def mask_of(order, degrees):
    shape = (order.shape[0], degrees)
    n = lax.broadcasted_iota(jnp.int32, shape, 1)
    sine = lax.broadcasted_iota(jnp.int32, shape, 0) & 1
    return (n <= LMAX) & (n >= jnp.maximum(order, 2)) & (order >= sine)


def eight(ref, g):
    return jnp.concatenate([ref[HALF * g + i] for i in range(HALF)], axis=0)


def chunks_of(rows):
    size = 512 if rows % 512 == 0 else rows
    return [(i, size) for i in range(0, rows, size)]


def packed_rows(rows, nodes):
    rest = nodes % LANES
    tall = -(-rows // (LANES // rest) // SUB) * SUB if rest else 0
    return rows * (nodes // LANES) + tall, tall


def pack(x, out_ref, at):
    rows, nodes = x.shape
    rest = nodes % LANES
    for i in range(nodes // LANES):
        out_ref[at + i * rows : at + (i + 1) * rows, :] = x[:, i * LANES : (i + 1) * LANES]
    tall = packed_rows(rows, nodes)[1]
    base = at + rows * (nodes // LANES)
    for i in range(-(-rows // tall) if rest else 0):
        top = min(tall, rows - i * tall)
        out_ref[base : base + top, i * rest : (i + 1) * rest] = x[i * tall : i * tall + top, nodes - rest :]


def unpack(ref, at, rows, nodes):
    rest = nodes % LANES
    parts = [ref[at + i * rows : at + (i + 1) * rows, :] for i in range(nodes // LANES)]
    tall = packed_rows(rows, nodes)[1]
    base = at + rows * (nodes // LANES)
    if rest:
        last = []
        for i in range(-(-rows // tall)):
            top = min(tall, rows - i * tall)
            last.append(ref[base : base + top, i * rest : (i + 1) * rest])
        parts.append(jnp.concatenate(last, axis=0))
    return jnp.concatenate(parts, axis=1)


def order_group(leg, g, x, dims):
    hi, lo = split2(x)
    x2 = jnp.concatenate([hi, lo], axis=0)
    sub = lax.broadcasted_iota(jnp.int32, x2.shape, 0) % SUB // 2
    total = None
    for i in range(HALF):
        term = mm(jnp.where(sub == i, x2, jnp.zeros_like(x2)), leg[g * HALF + i], dims)
        total = term if total is None else total + term
    return total[: x.shape[0]] + total[x.shape[0] :]


def nodal_of(leg, readers, nodal_ref):
    wide = 2 * leg.shape[0]
    for g in range(wide // SUB):
        y = order_group(leg, g, jnp.concatenate([read(g) for read in readers], axis=0), NT)
        for v in range(len(readers)):
            nodal_ref[v * wide + g * SUB : v * wide + (g + 1) * SUB, :] = y[v * SUB : (v + 1) * SUB]


def phase_at(phase_ref, at, size):
    tiles = range(at // LANES, (at + size) // LANES)
    return jnp.concatenate([phase_ref[t] for t in tiles], axis=1)


def rows_of(nodal_ref, phase_ref, data_ref, out_ref, count):
    nodes = nodal_ref.shape[1]
    wide = nodal_ref.shape[0] // count
    hi, lo = split2(nodal_ref[...])
    for at, size in chunks_of(data_ref.shape[1]):
        sel = one_hot(nodes, data_ref[NODE : NODE + 1, at : at + size].astype(jnp.int32))
        terms = mm(hi, sel) + mm(lo, sel)
        ph = phase_at(phase_ref, at, size)
        for v in range(count):
            part = terms[v * wide : (v + 1) * wide] * ph
            out_ref[v : v + 1, at : at + size] = jnp.sum(part, axis=0, keepdims=True)


def gather_nodes(u_list, phase_ref, data_ref, nodes):
    totals = [None] * len(u_list)
    for at, size in chunks_of(data_ref.shape[1]):
        sel = one_hot(nodes, data_ref[NODE : NODE + 1, at : at + size].astype(jnp.int32))
        ph = phase_at(phase_ref, at, size)
        for v, u in enumerate(u_list):
            hi, lo = split2(ph * u[:, at : at + size])
            term = mm(hi, sel, NT) + mm(lo, sel, NT)
            totals[v] = term if totals[v] is None else totals[v] + term
    return totals


def phase_kernel(nodes, slots, data_ref, phase_ref, last_ref, first_ref, order_ref):
    rows = data_ref.shape[1]
    lane = lax.broadcasted_iota(jnp.int32, (2 * slots, slots), 1)
    row = lax.broadcasted_iota(jnp.int32, (2 * slots, slots), 0)
    line = data_ref[ORDER : ORDER + 1, 0:slots]
    twice = jnp.sum(jnp.where(lane == row // 2, line, 0.0), axis=1, keepdims=True)
    order_ref[...] = twice.astype(jnp.int32)
    order = jnp.sum(jnp.where(lane[:slots] == row[:slots], line, 0.0), axis=1, keepdims=True)
    for at, size in chunks_of(rows):
        cos, sin = sincos(data_ref[LON : LON + 1, at : at + size] * order)
        for c, value in enumerate((cos, sin)):
            for t in range(size // LANES):
                tile = value[:, t * LANES : (t + 1) * LANES]
                phase_ref[at // LANES + t, pl.ds(c, slots, stride=2), :] = tile
    seg = data_ref[SEG : SEG + 1, :]
    first = jnp.min(seg, axis=1, keepdims=True)
    last = jnp.max(seg, axis=1, keepdims=True)
    w = data_ref[WEIGHT : WEIGHT + 1, :]
    parts = [jnp.where(seg == last, w, 0.0), jnp.where(seg == first, w, 0.0)]
    totals = gather_nodes(parts, phase_ref, data_ref, nodes)
    for out_ref, total, ident, part in zip((last_ref, first_ref), totals, (last, first), parts):
        pack(total, out_ref, 0)
        amount = jnp.sum(part, axis=1, keepdims=True)
        column = lax.broadcasted_iota(jnp.int32, (SUB, LANES), 1)
        out_ref[out_ref.shape[0] - SUB :, :] = jnp.where(column == 0, amount, ident + 1.0)


def blocks_kernel(pre_hbm, out_ref, pre, sem):
    copy = pltpu.make_async_copy(pre_hbm, pre, sem)
    copy.start()
    copy.wait()

    def one(l, carry):
        for g in range(out_ref.shape[1] // SUB):
            out_ref[l, g * SUB : (g + 1) * SUB, :] = eight(pre.at[l], g)
        return carry

    lax.fori_loop(0, out_ref.shape[0], one, 0)


def forward_kernel(phase_ref, data_ref, order_ref, x_ref, d_ref, leg, out_ref, nodal):
    degrees = x_ref.shape[2]

    def reader(ref):
        def read(g):
            keep = mask_of(order_ref[g * SUB : (g + 1) * SUB, :], degrees)
            return jnp.where(keep, eight(ref, g), 0.0)

        return read

    nodal_of(leg, [reader(x_ref), reader(d_ref)], nodal)
    rows_of(nodal, phase_ref, data_ref, out_ref, 2)


def centered(e_list, weight, seg, prev_row, next_row, segments):
    rows = seg.shape[1]
    ids = lax.broadcasted_iota(jnp.int32, (segments, rows), 0)
    sel = jnp.where(ids == seg, 1.0, 0.0).astype(BF16)
    stack = [weight] + [weight * e for e in e_list]
    pieces = [p for s in stack for p in split3(s)]
    fill = -len(pieces) % 16
    pieces = pieces + [jnp.zeros((fill, rows), BF16)] * (fill > 0)
    sums = mm(jnp.concatenate(pieces, axis=0), sel, NT)
    sums = [sums[3 * i : 3 * i + 1] + sums[3 * i + 1 : 3 * i + 2] + sums[3 * i + 2 : 3 * i + 3] for i in range(len(stack))]
    first = jnp.min(seg, axis=1, keepdims=True)
    last = jnp.max(seg, axis=1, keepdims=True)
    lane = lax.broadcasted_iota(jnp.int32, (1, segments), 1)
    at_first, at_last = lane == first, lane == last
    join_prev = jnp.where(prev_row[:, 1:2] == first.astype(F32) + 1.0, 1.0, 0.0)
    join_next = jnp.where(next_row[:, 1:2] == last.astype(F32) + 1.0, 1.0, 0.0)
    whole = sums[0]
    whole = whole + jnp.where(at_first, join_prev * prev_row[:, 0:1], 0.0)
    whole = whole + jnp.where(at_last, join_next * next_row[:, 0:1], 0.0)
    whole = jnp.where(whole > 0.0, whole, 1.0)
    means = [s / whole for s in sums[1:]]
    pieces = [p for m in means for p in split3(m)]
    fill = -len(pieces) % 16
    pieces = pieces + [jnp.zeros((fill, segments), BF16)]
    spread = mm(jnp.concatenate(pieces, axis=0), sel)
    out = []
    for i, m in enumerate(means):
        mean = spread[3 * i : 3 * i + 1] + spread[3 * i + 1 : 3 * i + 2] + spread[3 * i + 2 : 3 * i + 3]
        to_prev = join_prev * jnp.sum(jnp.where(at_first, m, 0.0), axis=1, keepdims=True)
        to_next = join_next * jnp.sum(jnp.where(at_last, m, 0.0), axis=1, keepdims=True)
        out.append((weight * (e_list[i] - mean), to_prev, to_next))
    return out


def center_and_gather(e_list, data_ref, phase_ref, prev_ref, next_ref, out_ref, segments, nodes):
    wide = phase_ref.shape[1]
    prev_row, next_row = (r[r.shape[0] - SUB : r.shape[0] - SUB + 1, :] for r in (prev_ref, next_ref))
    done = centered(e_list, data_ref[WEIGHT : WEIGHT + 1, :], data_ref[SEG : SEG + 1, :].astype(jnp.int32), prev_row, next_row, segments)
    totals = gather_nodes([u for u, _, _ in done], phase_ref, data_ref, nodes)
    tall = packed_rows(wide, nodes)[0]
    for v, (_, to_prev, to_next) in enumerate(done):
        pack(totals[v], out_ref, v * tall)
        part = slice(v * tall, (v + 1) * tall)
        out_ref[part, :] = out_ref[part, :] - to_prev * prev_ref[0:tall, :] - to_next * next_ref[0:tall, :]


def back_first_kernel(segments, nodes, p_ref, data_ref, phase_ref, prev_ref, next_ref, out_ref):
    e_list = [data_ref[GRAD : GRAD + 1, :] - p_ref[0:1, :], p_ref[1:2, :]]
    center_and_gather(e_list, data_ref, phase_ref, prev_ref, next_ref, out_ref, segments, nodes)


def steps_of(row):
    residual_dot, curvature, first, second = (row[:, i : i + 1] for i in range(4))
    step = residual_dot / curvature
    return step, (first - step * second) / curvature


def back_next_kernel(segments, nodes, p_ref, before_ref, data_ref, phase_ref, prev_ref, next_ref, out_ref):
    rows = data_ref.shape[1]
    step, beta = steps_of(p_ref[0:1, rows : rows + 4])
    e = p_ref[0:1, 0:rows] - step * p_ref[1:2, 0:rows] - beta * before_ref[1:2, :]
    center_and_gather([e], data_ref, phase_ref, prev_ref, next_ref, out_ref, segments, nodes)


def lifted(leg, gathered, store):
    for g in range(gathered[0].shape[0] // SUB):
        x = jnp.concatenate([v[g * SUB : (g + 1) * SUB, :] for v in gathered], axis=0)
        y = order_group(leg, g, x, NN)
        for v in range(len(gathered)):
            store(v, g, y[v * SUB : (v + 1) * SUB])


def precondition(pre, vectors_ref, out_ref):
    degrees = vectors_ref.shape[1]
    wide = pre.shape[1]
    lane = lax.broadcasted_iota(jnp.int32, (1, degrees), 1).astype(F32)
    start_row = (jnp.floor((lane + 0.5) * (1.0 / DB)) * DB).astype(jnp.int32)
    half = degrees // DB // 2 * DB
    base = half // LANES * LANES
    ends = (base + LANES) if half % LANES else half
    ends = min(ends, degrees)
    left = split2(vectors_ref[:, 0:half])
    right = split2(vectors_ref[:, half:])
    near = lax.broadcasted_iota(jnp.int32, (half, ends), 0) - start_row[:, 0:ends]
    far = lax.broadcasted_iota(jnp.int32, (degrees - half, degrees - base), 0) + half - start_row[:, base:]
    for l in range(DB):
        spread = jnp.where(near == l, 1.0, 0.0).astype(BF16)
        a = mm(left[0], spread) + mm(left[1], spread)
        spread = jnp.where(far == l, 1.0, 0.0).astype(BF16)
        b = mm(right[0], spread) + mm(right[1], spread)
        for at in range(0, vectors_ref.shape[0], wide):
            rows = slice(at, at + wide)
            pieces = [
                (slice(0, base), a[rows, 0:base]),
                (slice(base, ends), a[rows, base:ends] + b[rows, 0 : ends - base]),
                (slice(ends, degrees), b[rows, ends - base :]),
            ]
            for lanes, value in pieces:
                if lanes.stop == lanes.start:
                    continue
                term = pre[l, :, lanes] * value
                if l == 0:
                    out_ref[rows, lanes] = term
                else:
                    out_ref[rows, lanes] += term


def scalar_row(values, width):
    lane = lax.broadcasted_iota(jnp.int32, (1, width), 1)
    row = jnp.zeros((1, width), F32)
    for i, value in enumerate(values):
        row = jnp.where(lane == i, value, row)
    return row


def four_dots(pairs):
    sums = [jnp.sum(jnp.sum(a * b, axis=0, keepdims=True), axis=1, keepdims=True) for a, b in pairs]
    return sums


def middle_kernel(
    gathered_ref, phase_ref, data_ref, order_ref, kaula_ref, x_ref, d_ref, leg, pre,
    out_ref, r_ref, q_ref, pr_ref, pq_ref,
    nodal, vec, smooth,
):
    slots, degrees = x_ref.shape[0], x_ref.shape[2]
    nodes = nodal.shape[1]
    wide = 2 * slots
    rows = data_ref.shape[1]
    tall = packed_rows(wide, nodes)[0]

    def store(v, g, y):
        keep = mask_of(order_ref[g * SUB : (g + 1) * SUB, :], degrees)
        k = eight(kaula_ref, g)
        value = y - k * eight(x_ref, g) if v == 0 else y + k * eight(d_ref, g)
        vec[v * wide + g * SUB : v * wide + (g + 1) * SUB, :] = jnp.where(keep, value, 0.0)

    lifted(leg, [unpack(gathered_ref, v * tall, wide, nodes) for v in range(2)], store)
    precondition(pre, vec, smooth)
    keep = mask_of(order_ref[...], degrees)
    r, q = vec[0:wide, :], vec[wide:, :]
    pr = jnp.where(keep, smooth[0:wide, :], 0.0)
    pq = jnp.where(keep, smooth[wide:, :], 0.0)
    d = jnp.where(keep, jnp.concatenate([eight(d_ref, g) for g in range(wide // SUB)], axis=0), 0.0)
    smooth[0:wide, :] = pr
    smooth[wide:, :] = pq
    r_ref[...], q_ref[...], pr_ref[...], pq_ref[...] = r, q, pr, pq
    out_ref[0:1, rows:] = scalar_row(four_dots(((r, d), (d, q), (pr, q), (pq, q))), out_ref.shape[1] - rows)
    out_ref[1:2, rows:] = jnp.zeros((1, out_ref.shape[1] - rows), F32)

    def reader(v):
        return lambda g: smooth[v * wide + g * SUB : v * wide + (g + 1) * SUB, :]

    nodal_of(leg, [reader(0), reader(1)], nodal)
    rows_of(nodal, phase_ref, data_ref, out_ref, 2)


def last_kernel(
    gathered_ref, row_ref, order_ref, kaula_ref, d_ref, r_ref, q_ref, pr_ref, pq_ref, leg, pre,
    dots_ref, q1_ref, pq1_ref,
    d1, smooth,
):
    slots, degrees = d_ref.shape[0], d_ref.shape[2]
    wide = 2 * slots
    at = row_ref.shape[1] - LANES
    step, beta = steps_of(row_ref[0:1, at : at + 4])

    def store(v, g, y):
        part = slice(g * SUB, (g + 1) * SUB)
        keep = mask_of(order_ref[part, :], degrees)
        d = jnp.where(keep, eight(d_ref, g), 0.0)
        new = pr_ref[part, :] - step * pq_ref[part, :] - beta * d
        d1[part, :] = new
        q1_ref[part, :] = jnp.where(keep, y + eight(kaula_ref, g) * new, 0.0)

    nodes = leg.shape[1]
    lifted(leg, [unpack(gathered_ref, 0, wide, nodes)], store)
    precondition(pre, q1_ref, smooth)
    keep = mask_of(order_ref[...], degrees)
    q = q1_ref[...]
    pq = jnp.where(keep, smooth[...], 0.0)
    pq1_ref[...] = pq
    r1 = r_ref[...] - step * q_ref[...]
    pr1 = pr_ref[...] - step * pq_ref[...]
    d = d1[...]
    dots_ref[...] = scalar_row(four_dots(((r1, d), (d, q), (pr1, q), (pq, q))), dots_ref.shape[1])


def final_kernel(
    row_ref, dots_ref, order_ref, x_ref, d_ref, r_ref, q_ref, pr_ref, pq_ref, q1_ref, pq1_ref, ox_ref, or_ref, od_ref
):
    slots, degrees = x_ref.shape[0], x_ref.shape[2]
    at = row_ref.shape[1] - LANES
    step, beta = steps_of(row_ref[0:1, at : at + 4])
    step1, beta1 = steps_of(dots_ref[0:1, 0:4])
    for g in range(2 * slots // SUB):
        part = slice(g * SUB, (g + 1) * SUB)
        keep = mask_of(order_ref[part, :], degrees)
        d = jnp.where(keep, eight(d_ref, g), 0.0)
        pr1 = pr_ref[part, :] - step * pq_ref[part, :]
        d1 = pr1 - beta * d
        x2 = jnp.where(keep, eight(x_ref, g), 0.0) + step * d + step1 * d1
        r2 = r_ref[part, :] - step * q_ref[part, :] - step1 * q1_ref[part, :]
        d2 = pr1 - step1 * pq1_ref[part, :] - beta1 * d1
        for out_ref, value in ((ox_ref, x2), (or_ref, r2), (od_ref, d2)):
            for i in range(HALF):
                out_ref[HALF * g + i] = value[2 * i : 2 * i + 2]


def work(us):
    return pl.CostEstimate(flops=int(us * 1e9), bytes_accessed=int(us * 3e6), transcendentals=0)


def butterfly(x, axis):
    size = lax.axis_size(axis)
    step = 1
    while step < size:
        x = x + lax.ppermute(x, axis, [(i, i ^ step) for i in range(size)])
        step *= 2
    return x


def call(kernel, outs, scratch, n_in, hbm=False, cost=None):
    outs = [o if isinstance(o, jax.ShapeDtypeStruct) else jax.ShapeDtypeStruct(o, F32) for o in outs]
    return pl.pallas_call(
        kernel,
        out_shape=outs,
        in_specs=[HBM if hbm else VMEM] * n_in,
        out_specs=[VMEM for _ in outs],
        scratch_shapes=scratch,
        cost_estimate=cost,
        compiler_params=pltpu.CompilerParams(vmem_limit_bytes=LIMIT),
    )


def shards(longitude, node_index, weight, gradient, segment, order_map, legendre, precond, kaula, start, direction):
    rows = longitude.shape[0]
    slots, nodes, degrees = legendre.shape
    wide = 2 * slots
    tall = packed_rows(wide, nodes)[0]
    segments = lax.axis_size("tm") * lax.axis_size("order")
    kaula, start, direction = (v.transpose(1, 0, 2) for v in (kaula, start, direction))
    pre_all = precond.transpose(0, 2, 1, 3)
    coef = (wide, degrees)
    line = jnp.pad(order_map, (0, rows - slots))
    data = jnp.stack([v.astype(F32) for v in (longitude, node_index, weight, segment, gradient, line)])

    phase, last_edge, first_edge, order = call(
        functools.partial(phase_kernel, nodes, slots),
        [(rows // LANES, wide, LANES)] + [(tall + SUB, LANES)] * 2 + [jax.ShapeDtypeStruct((wide, 1), jnp.int32)],
        [],
        1,
        cost=work(4.0),
    )(data)
    size = lax.axis_size("tm")
    up = [(i, i + 1) for i in range(size - 1)]
    prev_edge = lax.ppermute(last_edge, "tm", up)
    next_edge = lax.ppermute(first_edge, "tm", [(b, a) for a, b in up])
    (pre_all,) = call(
        blocks_kernel,
        [(DB,) + coef],
        [pltpu.VMEM(pre_all.shape, F32), pltpu.SemaphoreType.DMA(())],
        1,
        hbm=True,
        cost=work(3.0),
    )(pre_all)

    (part,) = call(forward_kernel, [(2, rows)], [pltpu.VMEM((2 * wide, nodes), F32)], 6, cost=work(6.0))(
        phase, data, order, start, direction, legendre
    )
    first_rows = butterfly(part, "order")
    (part,) = call(functools.partial(back_first_kernel, segments, nodes), [(2 * tall, LANES)], [], 5, cost=work(2.0))(
        first_rows, data, phase, prev_edge, next_edge
    )
    gathered = butterfly(part, "tm")
    part, r0, q0, pr0, pq0 = call(
        middle_kernel,
        [(2, rows + LANES)] + [coef] * 4,
        [pltpu.VMEM((2 * wide, nodes), F32)] + [pltpu.VMEM((2 * wide, degrees), F32)] * 2,
        9,
        cost=work(10.0),
    )(gathered, phase, data, order, kaula, start, direction, legendre, pre_all)
    next_rows = butterfly(part, "order")
    (part,) = call(functools.partial(back_next_kernel, segments, nodes), [(tall, LANES)], [], 6, cost=work(2.0))(
        next_rows, first_rows, data, phase, prev_edge, next_edge
    )
    gathered = butterfly(part, "tm")
    dots, q1, pq1 = call(last_kernel, [(1, LANES)] + [coef] * 2, [pltpu.VMEM((wide, degrees), F32)] * 2, 11, cost=work(4.0))(
        gathered, next_rows, order, kaula, direction, r0, q0, pr0, pq0, legendre, pre_all
    )
    dots = butterfly(dots, "order")
    outs = call(final_kernel, [(slots, 2, degrees)] * 3, [], 11)(
        next_rows, dots, order, start, direction, r0, q0, pr0, pq0, q1, pq1
    )
    return tuple(o.transpose(1, 0, 2) for o in outs)


def solution(mesh):
    coef = P(None, "order", None)
    placed = (P("tm"),) * 5 + (P("order"), P("order", None, None), P(None, None, "order", None), coef, coef, coef)
    return jax.shard_map(shards, mesh=mesh, in_specs=placed, out_specs=(coef, coef, coef), check_vma=False)
```

time: 157 us -> 94.9 us (0.60)
  Pallas kernels: 59.6 us -> 32.5 us
  local copies, waits for them, and re-layouts: 16.3 us -> 0.93 us
  waiting for transfers between devices: 45.1 us -> 33.9 us
  other arithmetic: 9.02 us -> 2.28 us
  between operations: 4.06 us -> 0.83 us
  starting transfers between devices: 22 us -> 23.9 us
    pallas_call x6 -> x8, Pallas kernels: 59.6 us -> 32.5 us  [the longest x1 11 us: shards(): call(middle_kernel, [(2, rows + LANES)] + [coef] * 4, [pltpu.VMEM((2 * wi...]
    unnamed x13 -> x12, local copies, waits for them, and re-layouts: 12.1 us -> 0.04 us
    ppermute x12, waiting for transfers between devices: 45.1 us -> 33.9 us  [butterfly(): x = x + lax.ppermute(x, axis, [(i, i ^ step) for i in range(size)])]
    add x12, other arithmetic: 6.93 us -> 0.19 us  [butterfly(): x = x + lax.ppermute(x, axis, [(i, i ^ step) for i in range(size)])]
    ppermute x12, starting transfers between devices: 15 us -> 17.7 us  [butterfly(): x = x + lax.ppermute(x, axis, [(i, i ^ step) for i in range(size)])]
    convert_element_type x0 -> x3, other arithmetic: none -> 2.1 us  [shards(): v.astype(F32)]
    slice x2 -> x0, local copies, waits for them, and re-layouts: 1.78 us -> none  [the longest x1 1.18 us: shards(): row = lax.slice(next_rows, (0, rows), (1, rows + 128))]
  transfers between devices with their start and end apart: 14 -> 14, of which waited for: 12 -> 12; matrix products, arithmetic and copies ran while one was open for 8% -> 0% of each run, Pallas kernels for 9% -> 9%
where the time goes in v2:
time: 94.9 us; the launch traced here: 94.3 us
  waiting for transfers between devices  33.9 us (36%)
  Pallas kernels  32.5 us (34%)
  starting transfers between devices  23.9 us (25%)
  other arithmetic  2.28 us (2%)
    ppermute x12, waiting for transfers between devices, butterfly(): x = x + lax.ppermute(x, axis, [(i, i ^ step) for i in range(size)])  33.9 us
    ppermute x12, starting transfers between devices, butterfly(): x = x + lax.ppermute(x, axis, [(i, i ^ step) for i in range(size)])  17.7 us
    pallas_call x1, Pallas kernels, shards(): call(middle_kernel, [(2, rows + LANES)] + [coef] * 4, [pltpu.VMEM((2 * wi...  11 us
    pallas_call x1, Pallas kernels, shards(): call(forward_kernel, [(2, rows)], [pltpu.VMEM((2 * wide, nodes), F32)], 6...  5.9 us
    ppermute x1, starting transfers between devices, shards(): prev_edge = lax.ppermute(last_edge, 'tm', up)  4.91 us
    pallas_call x1, Pallas kernels, shards(): call(last_kernel, [(1, LANES)] + [coef] * 2, [pltpu.VMEM((wide, degrees),...  4.09 us
    pallas_call x1, Pallas kernels, shards(): call(functools.partial(phase_kernel, nodes, slots), [(rows // LANES, wide...  3.87 us
    pallas_call x1, Pallas kernels, shards(): call(functools.partial(back_first_kernel, segments, nodes), [(2 * tall, L...  2.33 us
  transfers between devices with their start and end apart: 14, of which 12 were waited for; matrix products, arithmetic and copies ran while one was open for 0% of the time, Pallas kernels for 9%

profile of v2, /device:TPU:0, one launch (start us, length us, event | category | flops | bytes accessed | tf_op | source)
XLA Modules:
  0.0 94.3 jit_solution(2345409259157236431)
XLA Ops:
  2.7 0.9 stack.27.data_ref
  3.7 3.9 %shard_map.130 = (f32[32,152,128]{2,1,0:T(8,128)S(1)}, f32[200,128]{1,0:T(8,128)S(1)}, f32[200,128]{1,0:T(8,128)S(1)}, s32[152,1]{1,0:T(8,128)S(1)}) custom-call(f32[6,4096]{1,0:T(8,128)S(1)} %stack.27.data_ref), custom_call_target="tpu_custom_call" | custom-call | flops 4000000000 | bytes 12000000 | tf_op jit(solution)/shard_map/pallas_call | solution.py:463
  7.5 4.9 %collective-permute-start.2 = (f32[200,128]{1,0:T(8,128)S(1)}, f32[200,128]{1,0:T(8,128)S(1)}, u32[]{:S(2)}, u32[]{:S(2)}) collective-permute-start(f32[200,128]{1,0:T(8,128)S(1)} %get-tuple-element.20), channel_id=1, source_target_pairs={{0,4},{4,8},{8,12},{12,16},{16,20},{20,24},{24,28},{1,5},{5,9},{9,... | collective-permute-start | bytes 307208 | tf_op jit(solution)/shard_map/ppermute | solution.py:472
  12.5 1.3 %collective-permute-start.3 = (f32[200,128]{1,0:T(8,128)S(1)}, f32[200,128]{1,0:T(8,128)S(1)}, u32[]{:S(2)}, u32[]{:S(2)}) collective-permute-start(f32[200,128]{1,0:T(8,128)S(1)} %get-tuple-element.21), channel_id=1, source_target_pairs={{4,0},{8,4},{12,8},{16,12},{20,16},{24,20},{28,24},{5,1},{9,5},{13... | collective-permute-start | bytes 307208 | tf_op jit(solution)/shard_map/ppermute | solution.py:473
  13.8 5.9 %shard_map.131 = f32[2,4096]{1,0:T(2,128)S(1)} custom-call(f32[32,152,128]{2,1,0:T(8,128)S(1)} %get-tuple-element.18.phase_ref, f32[6,4096]{1,0:T(8,128)S(1)} %stack.27.data_ref, s32[152,1]{1,0:T(8,128)S(1)} %get-tuple-element.19.order_ref, f32[76,2,304]{2,1,0:T(2,128)S(1)} %bitcast.19, f32[76,2,304]{2,1,0:T(2,128)S(1)} %bitcast.13, ...), custom_call_target="tpu_custom_call" | custom-call | flops 6000000000 | bytes 18000000 | tf_op jit(solution)/shard_map/pallas_call | solution.py:483
  19.8 1.2 %collective-permute-done = f32[2,4096]{1,0:T(2,128)S(1)} collective-permute-done((f32[2,4096]{1,0:T(2,128)S(1)}, f32[2,4096]{1,0:T(2,128)S(1)}, u32[]{:S(2)}, u32[]{:S(2)}) %collective-permute-start) | collective-permute-done | bytes 32800 | tf_op jit(solution)/shard_map/ppermute | solution.py:433
  21.0 1.6 %collective-permute-start.1 = (f32[2,4096]{1,0:T(2,128)S(1)}, f32[2,4096]{1,0:T(2,128)S(1)}, u32[]{:S(2)}, u32[]{:S(2)}) collective-permute-start(f32[2,4096]{1,0:T(2,128)S(1)} %add.38), channel_id=1, source_target_pairs={{0,2},{1,3},{2,0},{3,1},{4,6},{5,7},{6,4},{7,5},{8,10},{9,11},{10,... | collective-permute-start | bytes 98312 | tf_op jit(solution)/shard_map/ppermute | solution.py:433
  22.6 2.4 %collective-permute-done.1 = f32[2,4096]{1,0:T(2,128)S(1)} collective-permute-done((f32[2,4096]{1,0:T(2,128)S(1)}, f32[2,4096]{1,0:T(2,128)S(1)}, u32[]{:S(2)}, u32[]{:S(2)}) %collective-permute-start.1) | collective-permute-done | bytes 32800 | tf_op jit(solution)/shard_map/ppermute | solution.py:433
  25.0 2.3 %shard_map.132 = f32[384,128]{1,0:T(8,128)S(1)} custom-call(f32[2,4096]{1,0:T(2,128)S(1)} %add.39.p_ref.before_ref, f32[6,4096]{1,0:T(8,128)S(1)} %stack.27.data_ref, f32[32,152,128]{2,1,0:T(8,128)S(1)} %get-tuple-element.18.phase_ref, f32[200,128]{1,0:T(8,128)S(1)} %collective-permute-done.2.prev_ref, f32[200,128]{1,0:T(8,128)S(1)} %collective-permute-done.3.next_ref), custom_call_target="tpu_custom_call" | custom-call | flops 2000000000 | bytes 6000000 | tf_op jit(solution)/shard_map/pallas_call | solution.py:487
  27.4 2.7 %collective-permute-start.4 = (f32[384,128]{1,0:T(8,128)S(1)}, f32[384,128]{1,0:T(8,128)S(1)}, u32[]{:S(2)}, u32[]{:S(2)}) collective-permute-start(f32[384,128]{1,0:T(8,128)S(1)} %shard_map.132), channel_id=1, source_target_pairs={{0,4},{4,0},{8,12},{12,8},{16,20},{20,16},{24,28},{28,24},{1,5},{5... | collective-permute-start | bytes 589832 | tf_op jit(solution)/shard_map/ppermute | solution.py:433
  30.1 4.1 %collective-permute-done.4 = f32[384,128]{1,0:T(8,128)S(1)} collective-permute-done((f32[384,128]{1,0:T(8,128)S(1)}, f32[384,128]{1,0:T(8,128)S(1)}, u32[]{:S(2)}, u32[]{:S(2)}) %collective-permute-start.4) | collective-permute-done | bytes 196640 | tf_op jit(solution)/shard_map/ppermute | solution.py:433
  34.2 2.7 %collective-permute-start.5 = (f32[384,128]{1,0:T(8,128)S(1)}, f32[384,128]{1,0:T(8,128)S(1)}, u32[]{:S(2)}, u32[]{:S(2)}) collective-permute-start(f32[384,128]{1,0:T(8,128)S(1)} %add.40), channel_id=1, source_target_pairs={{0,8},{4,12},{8,0},{12,4},{16,24},{20,28},{24,16},{28,20},{1,9},{5... | collective-permute-start | bytes 589832 | tf_op jit(solution)/shard_map/ppermute | solution.py:433
  36.9 3.6 %collective-permute-done.5 = f32[384,128]{1,0:T(8,128)S(1)} collective-permute-done((f32[384,128]{1,0:T(8,128)S(1)}, f32[384,128]{1,0:T(8,128)S(1)}, u32[]{:S(2)}, u32[]{:S(2)}) %collective-permute-start.5) | collective-permute-done | bytes 196640 | tf_op jit(solution)/shard_map/ppermute | solution.py:433
  40.6 3.5 %collective-permute-start.6 = (f32[384,128]{1,0:T(8,128)S(1)}, f32[384,128]{1,0:T(8,128)S(1)}, u32[]{:S(2)}, u32[]{:S(2)}) collective-permute-start(f32[384,128]{1,0:T(8,128)S(1)} %add.41), channel_id=1, source_target_pairs={{0,16},{4,20},{8,24},{12,28},{16,0},{20,4},{24,8},{28,12},{1,17},{... | collective-permute-start | bytes 589832 | tf_op jit(solution)/shard_map/ppermute | solution.py:433
  44.1 2.2 %shard_map.133.pre = f32[19,152,304]{2,1,0:T(8,128)S(1)} custom-call(f32[19,76,2,304]{3,2,1,0:T(2,128)S(1)} %bitcast.24), custom_call_target="tpu_custom_call" | custom-call | flops 3000000000 | bytes 9000000 | tf_op jit(solution)/shard_map/pallas_call | solution.py:474
  46.3 3.7 %collective-permute-done.6 = f32[384,128]{1,0:T(8,128)S(1)} collective-permute-done((f32[384,128]{1,0:T(8,128)S(1)}, f32[384,128]{1,0:T(8,128)S(1)}, u32[]{:S(2)}, u32[]{:S(2)}) %collective-permute-start.6) | collective-permute-done | bytes 196640 | tf_op jit(solution)/shard_map/ppermute | solution.py:433
  50.0 11.0 %shard_map.134 = (f32[2,4224]{1,0:T(2,128)S(1)}, f32[152,304]{1,0:T(8,128)S(1)}, f32[152,304]{1,0:T(8,128)S(1)}, f32[152,304]{1,0:T(8,128)S(1)}, f32[152,304]{1,0:T(8,128)S(1)}) custom-call(f32[384,128]{1,0:T(8,128)S(1)} %add.42.gathered_ref, f32[32,152,128]{2,1,0:T(8,128)S(1)} %get-tuple-element.18.phase_ref, f32[6,4096]{1,0:T(8,128)S(1)} %stack.27.data_ref, ...), custom_call_target="tpu_custom_call" | custom-call | flops 10000000000 | bytes 30000000 | tf_op jit(solution)/shard_map/pallas_call | solution.py:491
  61.2 1.2 %collective-permute-done.7 = f32[2,4224]{1,0:T(2,128)S(1)} collective-permute-done((f32[2,4224]{1,0:T(2,128)S(1)}, f32[2,4224]{1,0:T(2,128)S(1)}, u32[]{:S(2)}, u32[]{:S(2)}) %collective-permute-start.7) | collective-permute-done | bytes 33824 | tf_op jit(solution)/shard_map/ppermute | solution.py:433
  62.4 1.5 %collective-permute-start.8 = (f32[2,4224]{1,0:T(2,128)S(1)}, f32[2,4224]{1,0:T(2,128)S(1)}, u32[]{:S(2)}, u32[]{:S(2)}) collective-permute-start(f32[2,4224]{1,0:T(2,128)S(1)} %add.43), channel_id=1, source_target_pairs={{0,2},{1,3},{2,0},{3,1},{4,6},{5,7},{6,4},{7,5},{8,10},{9,11},{10,... | collective-permute-start | bytes 101384 | tf_op jit(solution)/shard_map/ppermute | solution.py:433
  63.9 2.4 %collective-permute-done.8 = f32[2,4224]{1,0:T(2,128)S(1)} collective-permute-done((f32[2,4224]{1,0:T(2,128)S(1)}, f32[2,4224]{1,0:T(2,128)S(1)}, u32[]{:S(2)}, u32[]{:S(2)}) %collective-permute-start.8) | collective-permute-done | bytes 33824 | tf_op jit(solution)/shard_map/ppermute | solution.py:433
  66.4 1.8 %shard_map.135 = f32[192,128]{1,0:T(8,128)S(1)} custom-call(f32[2,4224]{1,0:T(2,128)S(1)} %add.44.p_ref.row_ref, f32[2,4096]{1,0:T(2,128)S(1)} %add.39.p_ref.before_ref, f32[6,4096]{1,0:T(8,128)S(1)} %stack.27.data_ref, f32[32,152,128]{2,1,0:T(8,128)S(1)} %get-tuple-element.18.phase_ref, f32[200,128]{1,0:T(8,128)S(1)} %collective-permute-done.2.prev_ref, ...), custom_call_target="tpu_custom_call" | custom-call | flops 2000000000 | bytes 6000000 | tf_op jit(solution)/shard_map/pallas_call | solution.py:499
  68.1 0.7 collective-permute-start.9
  68.9 4.0 %collective-permute-done.9 = f32[192,128]{1,0:T(8,128)S(1)} collective-permute-done((f32[192,128]{1,0:T(8,128)S(1)}, f32[192,128]{1,0:T(8,128)S(1)}, u32[]{:S(2)}, u32[]{:S(2)}) %collective-permute-start.9) | collective-permute-done | bytes 98336 | tf_op jit(solution)/shard_map/ppermute | solution.py:433
  72.8 0.8 collective-permute-start.10
  73.6 3.9 %collective-permute-done.10 = f32[192,128]{1,0:T(8,128)S(1)} collective-permute-done((f32[192,128]{1,0:T(8,128)S(1)}, f32[192,128]{1,0:T(8,128)S(1)}, u32[]{:S(2)}, u32[]{:S(2)}) %collective-permute-start.10) | collective-permute-done | bytes 98336 | tf_op jit(solution)/shard_map/ppermute | solution.py:433
  77.5 2.5 %collective-permute-start.11 = (f32[192,128]{1,0:T(8,128)S(1)}, f32[192,128]{1,0:T(8,128)S(1)}, u32[]{:S(2)}, u32[]{:S(2)}) collective-permute-start(f32[192,128]{1,0:T(8,128)S(1)} %add.46), channel_id=1, source_target_pairs={{0,16},{4,20},{8,24},{12,28},{16,0},{20,4},{24,8},{28,12},{1,17},{... | collective-permute-start | bytes 294920 | tf_op jit(solution)/shard_map/ppermute | solution.py:433
  80.0 4.2 %collective-permute-done.11 = f32[192,128]{1,0:T(8,128)S(1)} collective-permute-done((f32[192,128]{1,0:T(8,128)S(1)}, f32[192,128]{1,0:T(8,128)S(1)}, u32[]{:S(2)}, u32[]{:S(2)}) %collective-permute-start.11) | collective-permute-done | bytes 98336 | tf_op jit(solution)/shard_map/ppermute | solution.py:433
  84.2 4.1 %shard_map.136 = (f32[1,128]{1,0:T(1,128)S(1)}, f32[152,304]{1,0:T(8,128)S(1)}, f32[152,304]{1,0:T(8,128)S(1)}) custom-call(f32[192,128]{1,0:T(8,128)S(1)} %add.47.gathered_ref, f32[2,4224]{1,0:T(2,128)S(1)} %add.44.p_ref.row_ref, s32[152,1]{1,0:T(8,128)S(1)} %get-tuple-element.19.order_ref, f32[76,2,304]{2,1,0:T(2,128)S(1)} %bitcast.18, ...), custom_call_target="tpu_custom_call" | custom-call | flops 4000000000 | bytes 12000000 | tf_op jit(solution)/shard_map/pallas_call | solution.py:503
  88.3 1.2 %collective-permute-done.12 = f32[1,128]{1,0:T(1,128)S(1)} collective-permute-done((f32[1,128]{1,0:T(1,128)S(1)}, f32[1,128]{1,0:T(1,128)S(1)}, u32[]{:S(2)}, u32[]{:S(2)}) %collective-permute-start.12) | collective-permute-done | bytes 544 | tf_op jit(solution)/shard_map/ppermute | solution.py:433
  89.4 1.5 %collective-permute-start.13 = (f32[1,128]{1,0:T(1,128)S(1)}, f32[1,128]{1,0:T(1,128)S(1)}, u32[]{:S(2)}, u32[]{:S(2)}) collective-permute-start(f32[1,128]{1,0:T(1,128)S(1)} %add.48), channel_id=1, source_target_pairs={{0,2},{1,3},{2,0},{3,1},{4,6},{5,7},{6,4},{7,5},{8,10},{9,11},{10,... | collective-permute-start | bytes 1544 | tf_op jit(solution)/shard_map/ppermute | solution.py:433
  90.9 2.1 %collective-permute-done.13 = f32[1,128]{1,0:T(1,128)S(1)} collective-permute-done((f32[1,128]{1,0:T(1,128)S(1)}, f32[1,128]{1,0:T(1,128)S(1)}, u32[]{:S(2)}, u32[]{:S(2)}) %collective-permute-start.13) | collective-permute-done | bytes 544 | tf_op jit(solution)/shard_map/ppermute | solution.py:433
  93.0 1.3 %shard_map.137 = (f32[76,2,304]{2,1,0:T(2,128)}, f32[76,2,304]{2,1,0:T(2,128)}, f32[76,2,304]{2,1,0:T(2,128)}) custom-call(f32[2,4224]{1,0:T(2,128)S(1)} %add.44.p_ref.row_ref, f32[1,128]{1,0:T(1,128)S(1)} %add.49.dots_ref, s32[152,1]{1,0:T(8,128)S(1)} %get-tuple-element.19.order_ref, f32[76,2,304]{2,1,0:T(2,128)S(1)} %bitcast.21, ...), custom_call_target="tpu_custom_call" | custom-call | tf_op jit(solution)/shard_map/pallas_call | solution.py:507
  (33 shorter events, 2.5 us)
Async XLA Ops:
  3.6 10.1 %copy-start = (bf16[76,160,304]{2,1,0:T(8,128)(2,1)S(1)}, bf16[76,160,304]{2,1,0:T(8,128)(2,1)}, u32[]{:S(2)}) copy-start(bf16[76,160,304]{2,1,0:T(8,128)(2,1)} %leg.5) | copy-start | bytes 22179844
  3.6 10.1 %copy-start.1 = (f32[2,76,304]{2,0,1:T(2,128)S(1)}, f32[2,76,304]{2,0,1:T(2,128)}, u32[]{:S(2)}) copy-start(f32[2,76,304]{2,0,1:T(2,128)} %param.21) | copy-start | bytes 554500
  3.6 10.1 %copy-start.3 = (f32[2,76,304]{2,0,1:T(2,128)S(1)}, f32[2,76,304]{2,0,1:T(2,128)}, u32[]{:S(2)}) copy-start(f32[2,76,304]{2,0,1:T(2,128)} %param.20) | copy-start | bytes 554500
  7.5 17.5 %collective-permute-start.2 = (f32[200,128]{1,0:T(8,128)S(1)}, f32[200,128]{1,0:T(8,128)S(1)}, u32[]{:S(2)}, u32[]{:S(2)}) collective-permute-start(f32[200,128]{1,0:T(8,128)S(1)} %get-tuple-element.20), channel_id=1, source_target_pairs={{0,4},{4,8},{8,12},{12,16},{16,20},{20,24},{24,28},{1,5},{5,9},{9,... | collective-permute-start | bytes 307208 | tf_op jit(solution)/shard_map/ppermute | solution.py:472
  12.5 12.6 %collective-permute-start.3 = (f32[200,128]{1,0:T(8,128)S(1)}, f32[200,128]{1,0:T(8,128)S(1)}, u32[]{:S(2)}, u32[]{:S(2)}) collective-permute-start(f32[200,128]{1,0:T(8,128)S(1)} %get-tuple-element.21), channel_id=1, source_target_pairs={{4,0},{8,4},{12,8},{16,12},{20,16},{24,20},{28,24},{5,1},{9,5},{13... | collective-permute-start | bytes 307208 | tf_op jit(solution)/shard_map/ppermute | solution.py:473
  19.7 24.5 %slice-start = ((s8[4435968]{0:T(1024)(128)(4,1)}), s8[4194304]{0:T(1024)(128)(4,1)S(1)}, s32[]{:S(2)}) async-start(s8[4435968]{0:T(1024)(128)(4,1)} %bitcast.22), calls=%async_computation | async-start | bytes 8388608
  19.7 1.3 %collective-permute-start = (f32[2,4096]{1,0:T(2,128)S(1)}, f32[2,4096]{1,0:T(2,128)S(1)}, u32[]{:S(2)}, u32[]{:S(2)}) collective-permute-start(f32[2,4096]{1,0:T(2,128)S(1)} %shard_map.131), channel_id=1, source_target_pairs={{0,1},{1,0},{2,3},{3,2},{4,5},{5,4},{6,7},{7,6},{8,9},{9,8},{10,11... | collective-permute-start | bytes 98312 | tf_op jit(solution)/shard_map/ppermute | solution.py:433
  21.0 4.0 %collective-permute-start.1 = (f32[2,4096]{1,0:T(2,128)S(1)}, f32[2,4096]{1,0:T(2,128)S(1)}, u32[]{:S(2)}, u32[]{:S(2)}) collective-permute-start(f32[2,4096]{1,0:T(2,128)S(1)} %add.38), channel_id=1, source_target_pairs={{0,2},{1,3},{2,0},{3,1},{4,6},{5,7},{6,4},{7,5},{8,10},{9,11},{10,... | collective-permute-start | bytes 98312 | tf_op jit(solution)/shard_map/ppermute | solution.py:433
  25.0 19.1 %slice-start.1 = ((s8[4435968]{0:T(1024)(128)(4,1)}), s8[241664]{0:T(1024)(128)(4,1)S(1)}, s32[]{:S(2)}) async-start(s8[4435968]{0:T(1024)(128)(4,1)} %bitcast.22), calls=%async_computation.1 | async-start | bytes 483328
  27.4 6.8 %collective-permute-start.4 = (f32[384,128]{1,0:T(8,128)S(1)}, f32[384,128]{1,0:T(8,128)S(1)}, u32[]{:S(2)}, u32[]{:S(2)}) collective-permute-start(f32[384,128]{1,0:T(8,128)S(1)} %shard_map.132), channel_id=1, source_target_pairs={{0,4},{4,0},{8,12},{12,8},{16,20},{20,16},{24,28},{28,24},{1,5},{5... | collective-permute-start | bytes 589832 | tf_op jit(solution)/shard_map/ppermute | solution.py:433
  34.2 6.4 %collective-permute-start.5 = (f32[384,128]{1,0:T(8,128)S(1)}, f32[384,128]{1,0:T(8,128)S(1)}, u32[]{:S(2)}, u32[]{:S(2)}) collective-permute-start(f32[384,128]{1,0:T(8,128)S(1)} %add.40), channel_id=1, source_target_pairs={{0,8},{4,12},{8,0},{12,4},{16,24},{20,28},{24,16},{28,20},{1,9},{5... | collective-permute-start | bytes 589832 | tf_op jit(solution)/shard_map/ppermute | solution.py:433
  40.6 9.4 %collective-permute-start.6 = (f32[384,128]{1,0:T(8,128)S(1)}, f32[384,128]{1,0:T(8,128)S(1)}, u32[]{:S(2)}, u32[]{:S(2)}) collective-permute-start(f32[384,128]{1,0:T(8,128)S(1)} %add.41), channel_id=1, source_target_pairs={{0,16},{4,20},{8,24},{12,28},{16,0},{20,4},{24,8},{28,12},{1,17},{... | collective-permute-start | bytes 589832 | tf_op jit(solution)/shard_map/ppermute | solution.py:433
  44.1 5.9 %copy-start.2 = (f32[2,76,304]{2,0,1:T(2,128)S(1)}, f32[2,76,304]{2,0,1:T(2,128)}, u32[]{:S(2)}) copy-start(f32[2,76,304]{2,0,1:T(2,128)} %param.19) | copy-start | bytes 554500
  61.1 1.3 %collective-permute-start.7 = (f32[2,4224]{1,0:T(2,128)S(1)}, f32[2,4224]{1,0:T(2,128)S(1)}, u32[]{:S(2)}, u32[]{:S(2)}) collective-permute-start(f32[2,4224]{1,0:T(2,128)S(1)} %get-tuple-element.22), channel_id=1, source_target_pairs={{0,1},{1,0},{2,3},{3,2},{4,5},{5,4},{6,7},{7,6},{8,9},{9,8},{10,11... | collective-permute-start | bytes 101384 | tf_op jit(solution)/shard_map/ppermute | solution.py:433
  62.4 4.0 %collective-permute-start.8 = (f32[2,4224]{1,0:T(2,128)S(1)}, f32[2,4224]{1,0:T(2,128)S(1)}, u32[]{:S(2)}, u32[]{:S(2)}) collective-permute-start(f32[2,4224]{1,0:T(2,128)S(1)} %add.43), channel_id=1, source_target_pairs={{0,2},{1,3},{2,0},{3,1},{4,6},{5,7},{6,4},{7,5},{8,10},{9,11},{10,... | collective-permute-start | bytes 101384 | tf_op jit(solution)/shard_map/ppermute | solution.py:433
  68.1 4.7 %collective-permute-start.9 = (f32[192,128]{1,0:T(8,128)S(1)}, f32[192,128]{1,0:T(8,128)S(1)}, u32[]{:S(2)}, u32[]{:S(2)}) collective-permute-start(f32[192,128]{1,0:T(8,128)S(1)} %shard_map.135), channel_id=1, source_target_pairs={{0,4},{4,0},{8,12},{12,8},{16,20},{20,16},{24,28},{28,24},{1,5},{5... | collective-permute-start | bytes 294920 | tf_op jit(solution)/shard_map/ppermute | solution.py:433
  72.8 4.7 %collective-permute-start.10 = (f32[192,128]{1,0:T(8,128)S(1)}, f32[192,128]{1,0:T(8,128)S(1)}, u32[]{:S(2)}, u32[]{:S(2)}) collective-permute-start(f32[192,128]{1,0:T(8,128)S(1)} %add.45), channel_id=1, source_target_pairs={{0,8},{4,12},{8,0},{12,4},{16,24},{20,28},{24,16},{28,20},{1,9},{5... | collective-permute-start | bytes 294920 | tf_op jit(solution)/shard_map/ppermute | solution.py:433
  77.5 6.6 %collective-permute-start.11 = (f32[192,128]{1,0:T(8,128)S(1)}, f32[192,128]{1,0:T(8,128)S(1)}, u32[]{:S(2)}, u32[]{:S(2)}) collective-permute-start(f32[192,128]{1,0:T(8,128)S(1)} %add.46), channel_id=1, source_target_pairs={{0,16},{4,20},{8,24},{12,28},{16,0},{20,4},{24,8},{28,12},{1,17},{... | collective-permute-start | bytes 294920 | tf_op jit(solution)/shard_map/ppermute | solution.py:433
  88.3 1.2 %collective-permute-start.12 = (f32[1,128]{1,0:T(1,128)S(1)}, f32[1,128]{1,0:T(1,128)S(1)}, u32[]{:S(2)}, u32[]{:S(2)}) collective-permute-start(f32[1,128]{1,0:T(1,128)S(1)} %get-tuple-element.27), channel_id=1, source_target_pairs={{0,1},{1,0},{2,3},{3,2},{4,5},{5,4},{6,7},{7,6},{8,9},{9,8},{10,11... | collective-permute-start | bytes 1544 | tf_op jit(solution)/shard_map/ppermute | solution.py:433
  89.4 3.6 %collective-permute-start.13 = (f32[1,128]{1,0:T(1,128)S(1)}, f32[1,128]{1,0:T(1,128)S(1)}, u32[]{:S(2)}, u32[]{:S(2)}) collective-permute-start(f32[1,128]{1,0:T(1,128)S(1)} %add.48), channel_id=1, source_target_pairs={{0,2},{1,3},{2,0},{3,1},{4,6},{5,7},{6,4},{7,5},{8,10},{9,11},{10,... | collective-permute-start | bytes 1544 | tf_op jit(solution)/shard_map/ppermute | solution.py:433

commit v3 on v2

v3 whole, which is shorter than its diff:
```python
import functools

import jax
import jax.numpy as jnp
from jax import lax
from jax.experimental import pallas as pl
from jax.experimental.pallas import tpu as pltpu
from jax.sharding import PartitionSpec as P

LMAX = 300
DB = 19
SUB = 8
HALF = 4
LANES = 128
NODE, WEIGHT, SEG, GRAD, ODD = range(5)
F32 = jnp.float32
BF16 = jnp.bfloat16
NT = (((1,), (1,)), ((), ()))
NN = (((1,), (0,)), ((), ()))
VMEM = pl.BlockSpec(memory_space=pltpu.VMEM)
HBM = pl.BlockSpec(memory_space=pltpu.HBM)
LIMIT = 14 * 1024 * 1024


def mm(a, b, dims=NN):
    return lax.dot_general(a, b, dims, preferred_element_type=F32)


def split2(x):
    hi = x.astype(BF16)
    return hi, (x - hi.astype(F32)).astype(BF16)


def split3(x):
    hi = x.astype(BF16)
    rest = x - hi.astype(F32)
    mid = rest.astype(BF16)
    return hi, mid, (rest - mid.astype(F32)).astype(BF16)


def sincos(angle):
    quadrant = jnp.floor(angle * 0.6366197723675814 + 0.5)
    r = angle - quadrant * 1.5703125
    r = r - quadrant * 4.8351287841796875e-4
    r = r - quadrant * 3.1385570764541626e-7
    r = r - quadrant * 6.077100506506192e-11
    q = quadrant.astype(jnp.int32)
    z = r * r
    s = ((-1.9515295891e-4 * z + 8.3321608736e-3) * z - 1.6666654611e-1) * z * r + r
    c = ((2.443315711809948e-5 * z - 1.388731625493765e-3) * z + 4.166664568298827e-2) * z * z
    c = c - 0.5 * z + 1.0
    swap = (q & 1) == 1
    cos = jnp.where(swap, s, c)
    sin = jnp.where(swap, c, s)
    cos = jnp.where(((q + 1) & 2) == 2, -cos, cos)
    sin = jnp.where((q & 2) == 2, -sin, sin)
    return cos, sin


def one_hot(count, ids):
    rows = lax.broadcasted_iota(jnp.int32, (count, ids.shape[1]), 0)
    return jnp.where(rows == ids, 1.0, 0.0).astype(BF16)


def mask_of(order, degrees):
    shape = (order.shape[0], degrees)
    n = lax.broadcasted_iota(jnp.int32, shape, 1)
    sine = lax.broadcasted_iota(jnp.int32, shape, 0) & 1
    return (n <= LMAX) & (n >= jnp.maximum(order, 2)) & (order >= sine)


def eight(ref, g):
    return jnp.concatenate([ref[HALF * g + i] for i in range(HALF)], axis=0)


def chunks_of(rows):
    size = 512 if rows % 512 == 0 else rows
    return [(i, size) for i in range(0, rows, size)]


def packed_rows(rows, nodes):
    rest = nodes % LANES
    tall = -(-rows // (LANES // rest) // SUB) * SUB if rest else 0
    return rows * (nodes // LANES) + tall, tall


def pack(x, out_ref, at):
    rows, nodes = x.shape
    rest = nodes % LANES
    for i in range(nodes // LANES):
        out_ref[at + i * rows : at + (i + 1) * rows, :] = x[:, i * LANES : (i + 1) * LANES]
    tall = packed_rows(rows, nodes)[1]
    base = at + rows * (nodes // LANES)
    for i in range(-(-rows // tall) if rest else 0):
        top = min(tall, rows - i * tall)
        out_ref[base : base + top, i * rest : (i + 1) * rest] = x[i * tall : i * tall + top, nodes - rest :]


def unpack(ref, at, rows, nodes):
    rest = nodes % LANES
    parts = [ref[at + i * rows : at + (i + 1) * rows, :] for i in range(nodes // LANES)]
    tall = packed_rows(rows, nodes)[1]
    base = at + rows * (nodes // LANES)
    if rest:
        last = []
        for i in range(-(-rows // tall)):
            top = min(tall, rows - i * tall)
            last.append(ref[base : base + top, i * rest : (i + 1) * rest])
        parts.append(jnp.concatenate(last, axis=0))
    return jnp.concatenate(parts, axis=1)


def chunks_at(wide, nodes):
    cut = -(-wide // SUB // 2) * SUB
    out, at = [], 0
    for low, high in ((0, cut), (cut, wide)):
        out.append((low, high - low, at, packed_rows(high - low, nodes)[0]))
        at += out[-1][3]
    return out


def pack_all(x, ref):
    for low, count, at, _ in chunks_at(*x.shape):
        pack(x[low : low + count], ref, at)


def unpack_all(ref, wide, nodes):
    return jnp.concatenate([unpack(ref, at, count, nodes) for _, count, at, _ in chunks_at(wide, nodes)], axis=0)


def group_in(refs, g):
    cut = refs[0].shape[0] // SUB
    at, ref = (g, refs[0]) if g < cut else (g - cut, refs[1])
    return ref[at * SUB : (at + 1) * SUB, :]


def whole_of(refs):
    return jnp.concatenate([ref[...] for ref in refs], axis=0)


def order_group(table, g, x, dims):
    hi, lo = split2(x)
    x2 = jnp.concatenate([hi, lo], axis=0)
    sub = lax.broadcasted_iota(jnp.int32, x2.shape, 0) % SUB // 2
    total = None
    for i in range(HALF):
        term = mm(jnp.where(sub == i, x2, jnp.zeros_like(x2)), table(g * HALF + i), dims)
        total = term if total is None else total + term
    return total[: x.shape[0]] + total[x.shape[0] :]


def nodal_of(table, dims, wide, readers, nodal_ref, start=0):
    for g in range(wide // SUB):
        y = order_group(table, start + g, jnp.concatenate([read(g) for read in readers], axis=0), dims)
        for v in range(len(readers)):
            nodal_ref[v * wide + g * SUB : v * wide + (g + 1) * SUB, :] = y[v * SUB : (v + 1) * SUB]


def phase_at(phase_ref, at, size):
    tiles = range(at // LANES, (at + size) // LANES)
    return jnp.concatenate([phase_ref[t] for t in tiles], axis=1)


def rows_of(nodal, count, phase_ref, data_ref, out_ref):
    nodes = nodal.shape[1]
    wide = nodal.shape[0] // count
    hi, lo = split2(nodal)
    for at, size in chunks_of(data_ref.shape[1]):
        sel = one_hot(nodes, data_ref[NODE : NODE + 1, at : at + size].astype(jnp.int32))
        terms = mm(hi, sel) + mm(lo, sel)
        ph = phase_at(phase_ref, at, size)
        for v in range(count):
            part = terms[v * wide : (v + 1) * wide] * ph
            out_ref[v : v + 1, at : at + size] = jnp.sum(part, axis=0, keepdims=True)


def gather_nodes(u_list, phase_ref, data_ref, nodes):
    totals = [None] * len(u_list)
    for at, size in chunks_of(data_ref.shape[1]):
        sel = one_hot(nodes, data_ref[NODE : NODE + 1, at : at + size].astype(jnp.int32))
        ph = phase_at(phase_ref, at, size)
        for v, u in enumerate(u_list):
            hi, lo = split2(ph * u[:, at : at + size])
            term = mm(hi, sel, NT) + mm(lo, sel, NT)
            totals[v] = term if totals[v] is None else totals[v] + term
    return totals


def block_parts(degrees):
    step = 2 * LANES // (2 * DB) * DB
    spans = [(at, min(at + step, degrees)) for at in range(0, degrees, step)]
    return [(a, b, a // LANES * LANES, min(-(-b // LANES) * LANES, degrees)) for a, b in spans]


def spread_kernel(*refs):
    degrees = sum(ref.shape[1] for ref in refs) // 2
    for ref, (a, b, low, high) in zip(refs, block_parts(degrees)):
        lane = low + lax.broadcasted_iota(jnp.int32, (1, high - low), 1).astype(F32)
        start_row = (jnp.floor((lane + 0.5) * (1.0 / DB)) * DB).astype(jnp.int32)
        row = lax.broadcasted_iota(jnp.int32, (2 * (b - a), high - low), 0)
        source = a + jnp.where(row >= b - a, row - (b - a), row) - start_row
        for l in range(DB):
            ref[l] = jnp.where(source == l, 1.0, 0.0).astype(BF16)


def phase_kernel(
    nodes, odd_ref, line_ref, lon_ref, node_ref, weight_ref, seg_ref, grad_ref, near_ref,
    data_ref, phase_ref, pair_ref, cross_ref, order_ref,
):
    rows = data_ref.shape[1]
    slots = line_ref.shape[1]
    odd = jnp.broadcast_to(odd_ref[0:1, 0:1], (1, 1)) > 0
    for at, ref in ((NODE, node_ref), (WEIGHT, weight_ref), (SEG, seg_ref), (GRAD, grad_ref)):
        data_ref[at : at + 1, :] = ref[...].astype(F32)
    data_ref[ODD : ODD + 1, :] = jnp.broadcast_to(jnp.where(odd, 1.0, 0.0), (1, rows))
    lane = lax.broadcasted_iota(jnp.int32, (2 * slots, slots), 1)
    row = lax.broadcasted_iota(jnp.int32, (2 * slots, slots), 0)
    line = line_ref[...].astype(F32)
    twice = jnp.sum(jnp.where(lane == row // 2, line, 0.0), axis=1, keepdims=True)
    order_ref[...] = twice.astype(jnp.int32)
    order = jnp.sum(jnp.where(lane[:slots] == row[:slots], line, 0.0), axis=1, keepdims=True)
    for at, size in chunks_of(rows):
        cos, sin = sincos(lon_ref[:, at : at + size] * order)
        for c, value in enumerate((cos, sin)):
            for t in range(size // LANES):
                tile = value[:, t * LANES : (t + 1) * LANES]
                phase_ref[at // LANES + t, pl.ds(c, slots, stride=2), :] = tile
    w, at_pair, at_cross = data_ref[WEIGHT : WEIGHT + 1, :], *edge_ids(data_ref)
    idents = (at_pair, at_cross)
    parts = [jnp.where(data_ref[SEG : SEG + 1, :] == ident, w, 0.0) for ident in idents]
    totals = gather_nodes(parts, phase_ref, data_ref, nodes)
    for out_ref, total, ident, part in zip((pair_ref, cross_ref), totals, idents, parts):
        pack_all(total, out_ref)
        amount = jnp.sum(part, axis=1, keepdims=True)
        column = lax.broadcasted_iota(jnp.int32, (SUB, LANES), 1)
        out_ref[out_ref.shape[0] - SUB :, :] = jnp.where(column == 0, amount, ident + 1.0)


def edge_ids(data_ref):
    seg = data_ref[SEG : SEG + 1, :]
    first = jnp.min(seg, axis=1, keepdims=True)
    last = jnp.max(seg, axis=1, keepdims=True)
    odd = data_ref[ODD : ODD + 1, 0:1] > 0
    return jnp.where(odd, first, last), jnp.where(odd, last, first)


def blocks_kernel(pre_hbm, out_ref, pre, sem):
    copy = pltpu.make_async_copy(pre_hbm, pre, sem)
    copy.start()
    copy.wait()

    def one(l, carry):
        for g in range(out_ref.shape[1] // SUB):
            out_ref[l, g * SUB : (g + 1) * SUB, :] = eight(pre.at[l], g)
        return carry

    lax.fori_loop(0, out_ref.shape[0], one, 0)


def forward_kernel(phase_ref, data_ref, order_ref, x_ref, d_ref, leg, out_ref, nodal):
    degrees = x_ref.shape[2]

    def reader(ref):
        def read(g):
            keep = mask_of(order_ref[g * SUB : (g + 1) * SUB, :], degrees)
            return jnp.where(keep, eight(ref, g), 0.0)

        return read

    nodal_of(lambda m: leg[m], NT, 2 * leg.shape[0], [reader(x_ref), reader(d_ref)], nodal)
    rows_of(nodal[...], 2, phase_ref, data_ref, out_ref)


def centered(e_list, weight, seg, idents, rows_beside, segments):
    rows = seg.shape[1]
    ids = lax.broadcasted_iota(jnp.int32, (segments, rows), 0)
    sel = jnp.where(ids == seg, 1.0, 0.0).astype(BF16)
    stack = [weight] + [weight * e for e in e_list]
    pieces = [p for s in stack for p in split3(s)]
    fill = -len(pieces) % 16
    pieces = pieces + [jnp.zeros((fill, rows), BF16)] * (fill > 0)
    sums = mm(jnp.concatenate(pieces, axis=0), sel, NT)
    sums = [sums[3 * i : 3 * i + 1] + sums[3 * i + 1 : 3 * i + 2] + sums[3 * i + 2 : 3 * i + 3] for i in range(len(stack))]
    lane = lax.broadcasted_iota(jnp.int32, (1, segments), 1).astype(F32)
    whole, edges = sums[0], []
    for ident, row in zip(idents, rows_beside):
        join = jnp.where(row[:, 1:2] == ident + 1.0, 1.0, 0.0)
        edges.append((lane == ident, join))
        whole = whole + jnp.where(lane == ident, join * row[:, 0:1], 0.0)
    whole = jnp.where(whole > 0.0, whole, 1.0)
    means = [s / whole for s in sums[1:]]
    pieces = [p for m in means for p in split3(m)]
    fill = -len(pieces) % 16
    pieces = pieces + [jnp.zeros((fill, segments), BF16)]
    spread = mm(jnp.concatenate(pieces, axis=0), sel)
    out = []
    for i, m in enumerate(means):
        mean = spread[3 * i : 3 * i + 1] + spread[3 * i + 1 : 3 * i + 2] + spread[3 * i + 2 : 3 * i + 3]
        beside = [join * jnp.sum(jnp.where(at, m, 0.0), axis=1, keepdims=True) for at, join in edges]
        out.append((weight * (e_list[i] - mean), beside))
    return out


def center_and_gather(e_list, data_ref, phase_ref, pair_ref, cross_ref, out_refs, segments, nodes):
    wide = phase_ref.shape[1]
    chunks = chunks_at(wide, nodes)
    tall = sum(c[3] for c in chunks)
    beside_refs = (pair_ref, cross_ref)
    rows_beside = [r[tall : tall + 1, :] for r in beside_refs]
    weight, seg = data_ref[WEIGHT : WEIGHT + 1, :], data_ref[SEG : SEG + 1, :].astype(jnp.int32)
    done = centered(e_list, weight, seg, edge_ids(data_ref), rows_beside, segments)
    totals = gather_nodes([u for u, _ in done], phase_ref, data_ref, nodes)
    for v, (_, factors) in enumerate(done):
        for i, (low, count, at, high) in enumerate(chunks):
            out_ref, base = (out_refs[0], at) if len(out_refs) == 1 else (out_refs[i], v * high)
            pack(totals[v][low : low + count], out_ref, base)
            part = slice(base, base + high)
            for factor, ref in zip(factors, beside_refs):
                out_ref[part, :] = out_ref[part, :] - factor * ref[at : at + high, :]


def back_first_kernel(segments, nodes, p_ref, data_ref, phase_ref, pair_ref, cross_ref, *out_refs):
    e_list = [data_ref[GRAD : GRAD + 1, :] - p_ref[0:1, :], p_ref[1:2, :]]
    center_and_gather(e_list, data_ref, phase_ref, pair_ref, cross_ref, out_refs, segments, nodes)


def steps_of(row):
    residual_dot, curvature, first, second = (row[:, i : i + 1] for i in range(4))
    step = residual_dot / curvature
    return step, (first - step * second) / curvature


def back_next_kernel(segments, nodes, p_ref, before_ref, data_ref, phase_ref, pair_ref, cross_ref, out_ref):
    rows = data_ref.shape[1]
    step, beta = steps_of(p_ref[0:1, rows : rows + 4])
    e = p_ref[0:1, 0:rows] - step * p_ref[1:2, 0:rows] - beta * before_ref[1:2, :]
    center_and_gather([e], data_ref, phase_ref, pair_ref, cross_ref, [out_ref], segments, nodes)


def lifted(leg, gathered, store, start=0):
    for g in range(gathered[0].shape[0] // SUB):
        x = jnp.concatenate([v[g * SUB : (g + 1) * SUB, :] for v in gathered], axis=0)
        y = order_group(lambda m: leg[m], start + g, x, NN)
        for v in range(len(gathered)):
            store(v, g, y[v * SUB : (v + 1) * SUB])


def precondition(pre, tables, vectors_ref, out_ref, first=0, count=None):
    degrees = vectors_ref.shape[1]
    wide = count or pre.shape[1]
    hi, lo = split2(vectors_ref[...])
    parts = block_parts(degrees)
    pairs = [jnp.concatenate([hi[:, a:b], lo[:, a:b]], axis=1) for a, b, _, _ in parts]
    for l in range(DB):
        each = [mm(pair, table[l]) for pair, table in zip(pairs, tables)]
        for at in range(0, degrees, LANES):
            end = min(at + LANES, degrees)
            value = None
            for term, (_, _, low, high) in zip(each, parts):
                if low <= at and end <= high:
                    term = term[:, at - low : end - low]
                    value = term if value is None else value + term
            for top in range(0, vectors_ref.shape[0], wide):
                term = pre[l, first : first + wide, at:end] * value[top : top + wide]
                if l == 0:
                    out_ref[top : top + wide, at:end] = term
                else:
                    out_ref[top : top + wide, at:end] += term


def scalar_row(values, width):
    lane = lax.broadcasted_iota(jnp.int32, (1, width), 1)
    row = jnp.zeros((1, width), F32)
    for i, value in enumerate(values):
        row = jnp.where(lane == i, value, row)
    return row


def four_dots(pairs):
    sums = [jnp.sum(jnp.sum(a * b, axis=0, keepdims=True), axis=1, keepdims=True) for a, b in pairs]
    return sums


def middle_kernel(start, gathered_ref, order_ref, kaula_ref, x_ref, d_ref, leg, pre, *refs):
    tables, refs = refs[:-8], refs[-8:]
    nodal, dots_ref, r_ref, q_ref, pr_ref, pq_ref, vec, smooth = refs
    degrees = x_ref.shape[2]
    nodes = nodal.shape[1]
    wide = r_ref.shape[0]
    low = start * SUB
    tall = packed_rows(wide, nodes)[0]

    def store(v, g, y):
        keep = mask_of(order_ref[low + g * SUB : low + (g + 1) * SUB, :], degrees)
        k = eight(kaula_ref, start + g)
        value = y - k * eight(x_ref, start + g) if v == 0 else y + k * eight(d_ref, start + g)
        vec[v * wide + g * SUB : v * wide + (g + 1) * SUB, :] = jnp.where(keep, value, 0.0)

    lifted(leg, [unpack(gathered_ref, v * tall, wide, nodes) for v in range(2)], store, start)
    precondition(pre, tables, vec, smooth, low, wide)
    keep = mask_of(order_ref[low : low + wide, :], degrees)
    r, q = vec[0:wide, :], vec[wide:, :]
    pr = jnp.where(keep, smooth[0:wide, :], 0.0)
    pq = jnp.where(keep, smooth[wide:, :], 0.0)
    d = jnp.where(keep, jnp.concatenate([eight(d_ref, start + g) for g in range(wide // SUB)], axis=0), 0.0)
    smooth[0:wide, :] = pr
    smooth[wide:, :] = pq
    r_ref[...], q_ref[...], pr_ref[...], pq_ref[...] = r, q, pr, pq
    dots_ref[...] = scalar_row(four_dots(((r, d), (d, q), (pr, q), (pq, q))), dots_ref.shape[1])

    def reader(v):
        return lambda g: smooth[v * wide + g * SUB : v * wide + (g + 1) * SUB, :]

    nodal_of(lambda m: leg[m], NT, wide, [reader(0), reader(1)], nodal, start)


def middle_rows_kernel(first_ref, second_ref, dots_a, dots_b, phase_ref, data_ref, out_ref):
    rows = data_ref.shape[1]
    parts = []
    for v in range(2):
        for ref in (first_ref, second_ref):
            half = ref.shape[0] // 2
            parts.append(ref[v * half : (v + 1) * half, :])
    out_ref[0:1, rows:] = dots_a[...] + dots_b[...]
    out_ref[1:2, rows:] = jnp.zeros((1, out_ref.shape[1] - rows), F32)
    rows_of(jnp.concatenate(parts, axis=0), 2, phase_ref, data_ref, out_ref)


def last_kernel(gathered_ref, row_ref, order_ref, kaula_ref, d_ref, *refs):
    r_refs, q_refs, pr_refs, pq_refs = (refs[i : i + 2] for i in range(0, 8, 2))
    leg, pre, tables, refs = refs[8], refs[9], refs[10:-5], refs[-5:]
    dots_ref, q1_ref, pq1_ref, d1, smooth = refs
    slots, degrees = d_ref.shape[0], d_ref.shape[2]
    wide = 2 * slots
    at = row_ref.shape[1] - LANES
    step, beta = steps_of(row_ref[0:1, at : at + 4])

    def store(v, g, y):
        part = slice(g * SUB, (g + 1) * SUB)
        keep = mask_of(order_ref[part, :], degrees)
        d = jnp.where(keep, eight(d_ref, g), 0.0)
        new = group_in(pr_refs, g) - step * group_in(pq_refs, g) - beta * d
        d1[part, :] = new
        q1_ref[part, :] = jnp.where(keep, y + eight(kaula_ref, g) * new, 0.0)

    nodes = leg.shape[1]
    lifted(leg, [unpack_all(gathered_ref, wide, nodes)], store)
    precondition(pre, tables, q1_ref, smooth)
    keep = mask_of(order_ref[...], degrees)
    q = q1_ref[...]
    pq = jnp.where(keep, smooth[...], 0.0)
    pq1_ref[...] = pq
    r1 = whole_of(r_refs) - step * whole_of(q_refs)
    pr1 = whole_of(pr_refs) - step * whole_of(pq_refs)
    d = d1[...]
    dots_ref[...] = scalar_row(four_dots(((r1, d), (d, q), (pr1, q), (pq, q))), dots_ref.shape[1])


def final_kernel(row_ref, dots_ref, order_ref, x_ref, d_ref, *refs):
    r_refs, q_refs, pr_refs, pq_refs = (refs[i : i + 2] for i in range(0, 8, 2))
    q1_ref, pq1_ref, ox_ref, or_ref, od_ref = refs[8:]
    slots, degrees = x_ref.shape[0], x_ref.shape[2]
    at = row_ref.shape[1] - LANES
    step, beta = steps_of(row_ref[0:1, at : at + 4])
    step1, beta1 = steps_of(dots_ref[0:1, 0:4])
    for g in range(2 * slots // SUB):
        part = slice(g * SUB, (g + 1) * SUB)
        keep = mask_of(order_ref[part, :], degrees)
        d = jnp.where(keep, eight(d_ref, g), 0.0)
        pr1 = group_in(pr_refs, g) - step * group_in(pq_refs, g)
        d1 = pr1 - beta * d
        x2 = jnp.where(keep, eight(x_ref, g), 0.0) + step * d + step1 * d1
        r2 = group_in(r_refs, g) - step * group_in(q_refs, g) - step1 * q1_ref[part, :]
        d2 = pr1 - step1 * pq1_ref[part, :] - beta1 * d1
        for out_ref, value in ((ox_ref, x2), (or_ref, r2), (od_ref, d2)):
            for i in range(HALF):
                out_ref[HALF * g + i] = value[2 * i : 2 * i + 2]


def work(us):
    return pl.CostEstimate(flops=int(us * 1e9), bytes_accessed=int(us * 3e6), transcendentals=0)


def steps_over(axis):
    size = lax.axis_size(axis)
    return [1 << i for i in range(size.bit_length() - 1)]


def exchanged(x, axis, step):
    return x + lax.ppermute(x, axis, [(i, i ^ step) for i in range(lax.axis_size(axis))])


def butterfly(x, axis):
    for step in steps_over(axis):
        x = exchanged(x, axis, step)
    return x


def butterflies(first, second, axis):
    steps = steps_over(axis)
    for a, b in zip(steps, steps[1:] + steps[:1]):
        first, second = exchanged(first, axis, a), exchanged(second, axis, b)
    return first, second


def call(kernel, outs, scratch, n_in, hbm=False, cost=None):
    outs = [o if isinstance(o, jax.ShapeDtypeStruct) else jax.ShapeDtypeStruct(o, F32) for o in outs]
    return pl.pallas_call(
        kernel,
        out_shape=outs,
        in_specs=[HBM if hbm else VMEM] * n_in,
        out_specs=[VMEM for _ in outs],
        scratch_shapes=scratch,
        cost_estimate=cost,
        compiler_params=pltpu.CompilerParams(vmem_limit_bytes=LIMIT),
    )


def shards(longitude, node_index, weight, gradient, segment, order_map, legendre, precond, kaula, start, direction):
    rows = longitude.shape[0]
    slots, nodes, degrees = legendre.shape
    wide = 2 * slots
    chunks = chunks_at(wide, nodes)
    tall = sum(c[3] for c in chunks)
    segments = lax.axis_size("tm") * lax.axis_size("order")
    kaula, start, direction = (v.transpose(1, 0, 2) for v in (kaula, start, direction))
    pre_all = precond.transpose(0, 2, 1, 3)
    coef = (wide, degrees)
    shapes = [(DB, 2 * (b - a), high - low) for a, b, low, high in block_parts(degrees)]
    tables = call(spread_kernel, [jax.ShapeDtypeStruct(t, BF16) for t in shapes], [], 0, cost=work(4.0))()
    odd = (lax.axis_index("tm") % 2).reshape(1, 1)
    line = [v.reshape(1, -1) for v in (order_map, longitude, node_index, weight, segment, gradient)]
    data, phase, pair_edge, cross_edge, order = call(
        functools.partial(phase_kernel, nodes),
        [(SUB, rows), (rows // LANES, wide, LANES)] + [(tall + SUB, LANES)] * 2 + [jax.ShapeDtypeStruct((wide, 1), jnp.int32)],
        [],
        8,
        cost=work(4.0),
    )(odd, *line, tables[0])
    size = lax.axis_size("tm")
    pair_edge = lax.ppermute(pair_edge, "tm", [(i, i ^ 1) for i in range(size)])
    cross = [(i, i + 1) for i in range(1, size - 1, 2)]
    cross_edge = lax.ppermute(cross_edge, "tm", cross + [(b, a) for a, b in cross])
    (pre_all,) = call(
        blocks_kernel,
        [(DB,) + coef],
        [pltpu.VMEM(pre_all.shape, F32), pltpu.SemaphoreType.DMA(())],
        1,
        hbm=True,
        cost=work(3.0),
    )(pre_all)

    (part,) = call(forward_kernel, [(2, rows)], [pltpu.VMEM((2 * wide, nodes), F32)], 6, cost=work(6.0))(
        phase, data, order, start, direction, legendre
    )
    first_rows = butterfly(part, "order")
    first_rows, pre_all = lax.optimization_barrier((first_rows, pre_all))
    parts = call(
        functools.partial(back_first_kernel, segments, nodes), [(2 * c[3], LANES) for c in chunks], [], 5, cost=work(2.0)
    )(first_rows, data, phase, pair_edge, cross_edge)
    middle = [
        call(
            functools.partial(middle_kernel, low // SUB),
            [(2 * count, nodes), (1, LANES)] + [(count, degrees)] * 4,
            [pltpu.VMEM((2 * count, degrees), F32)] * 2,
            7 + len(tables),
            cost=work(4.0),
        )(gathered, order, kaula, start, direction, legendre, pre_all, *tables)
        for (low, count, _, _), gathered in zip(chunks, butterflies(*parts, "tm"))
    ]
    (nodal_a, dots_a, *halves_a), (nodal_b, dots_b, *halves_b) = middle
    state = [v for pair in zip(halves_a, halves_b) for v in pair]
    (part,) = call(middle_rows_kernel, [(2, rows + LANES)], [], 6, cost=work(2.0))(
        nodal_a, nodal_b, dots_a, dots_b, phase, data
    )
    next_rows = butterfly(part, "order")
    (part,) = call(functools.partial(back_next_kernel, segments, nodes), [(tall, LANES)], [], 6, cost=work(2.0))(
        next_rows, first_rows, data, phase, pair_edge, cross_edge
    )
    gathered = butterfly(part, "tm")
    dots, q1, pq1 = call(last_kernel, [(1, LANES)] + [coef] * 2, [pltpu.VMEM((wide, degrees), F32)] * 2, 15 + len(tables), cost=work(4.0))(
        gathered, next_rows, order, kaula, direction, *state, legendre, pre_all, *tables
    )
    dots = butterfly(dots, "order")
    outs = call(final_kernel, [(slots, 2, degrees)] * 3, [], 15)(
        next_rows, dots, order, start, direction, *state, q1, pq1
    )
    return tuple(o.transpose(1, 0, 2) for o in outs)


def solution(mesh):
    coef = P(None, "order", None)
    placed = (P("tm"),) * 5 + (P("order"), P("order", None, None), P(None, None, "order", None), coef, coef, coef)
    return jax.shard_map(shards, mesh=mesh, in_specs=placed, out_specs=(coef, coef, coef), check_vma=False)
```

time: 94.9 us -> 84 us (0.89)
  waiting for transfers between devices: 33.9 us -> 19.2 us
  starting transfers between devices: 23.9 us -> 30 us
  other arithmetic: 2.28 us -> 0.23 us
    ppermute x14 -> x17, waiting for transfers between devices: 33.9 us -> 19.2 us  [the longest x15 19.2 us: exchanged(): lax.ppermute(x, axis, [(i, i ^ step) for i in range(lax.axis_size(axis))])]
    ppermute x14 -> x17, starting transfers between devices: 23.9 us -> 30 us  [the longest x15 26.7 us: exchanged(): lax.ppermute(x, axis, [(i, i ^ step) for i in range(lax.axis_size(axis))])]
    convert_element_type x3 -> x0, other arithmetic: 2.1 us -> none  [shards(): v.astype(F32)]
    unnamed x12 -> x28, local copies, waits for them, and re-layouts: 0.04 us -> 1.22 us
    pallas_call x4 -> x7, Pallas kernels: 18.5 us -> 18.6 us  [the longest x2 8.54 us: shards(): call(functools.partial(middle_kernel, low // SUB), [(2 * count, nodes), (...]
  transfers between devices with their start and end apart: 14 -> 17, of which waited for: 12 -> 12; matrix products, arithmetic and copies ran while one was open for 0% -> 0% of each run, Pallas kernels for 9% -> 7%
where the time goes in v3:
time: 84 us; the launch traced here: 83.8 us
  Pallas kernels  32.3 us (38%)
  starting transfers between devices  30 us (36%)
  waiting for transfers between devices  19.2 us (23%)
  local copies, waits for them, and re-layouts  1.22 us (1%)
  between operations  0.96 us (1%)
    ppermute x15, starting transfers between devices, exchanged(): lax.ppermute(x, axis, [(i, i ^ step) for i in range(lax.axis_size(axis))])  26.7 us
    ppermute x15, waiting for transfers between devices, exchanged(): lax.ppermute(x, axis, [(i, i ^ step) for i in range(lax.axis_size(axis))])  19.2 us
    pallas_call x2, Pallas kernels, shards(): call(functools.partial(middle_kernel, low // SUB), [(2 * count, nodes), (...  8.54 us
    pallas_call x1, Pallas kernels, shards(): call(forward_kernel, [(2, rows)], [pltpu.VMEM((2 * wide, nodes), F32)], 6...  5.9 us
    pallas_call x1, Pallas kernels, shards(): call(functools.partial(phase_kernel, nodes), [(SUB, rows), (rows // LANES...  3.88 us
    pallas_call x1, Pallas kernels, shards(): call(last_kernel, [(1, LANES)] + [coef] * 2, [pltpu.VMEM((wide, degrees),...  3.61 us
    ppermute x1, starting transfers between devices, shards(): pair_edge = lax.ppermute(pair_edge, 'tm', [(i, i ^ 1) for i in range(size)])  2.58 us
    pallas_call x1, Pallas kernels, shards(): call(functools.partial(back_first_kernel, segments, nodes), [(2 * c[3], L...  2.31 us
  transfers between devices with their start and end apart: 17, of which 12 were waited for; matrix products, arithmetic and copies ran while one was open for 0% of the time, Pallas kernels for 7%

profile of v3, /device:TPU:0, one launch (start us, length us, event | category | flops | bytes accessed | tf_op | source)
XLA Modules:
  0.0 83.8 jit_solution(14897193293277897166)
XLA Ops:
  1.5 1.1 %copy-done.1 = bf16[19,152,176]{2,1,0:T(8,128)(2,1)} copy-done((bf16[19,152,176]{2,1,0:T(8,128)(2,1)}, bf16[19,152,176]{2,1,0:T(8,128)(2,1)S(1)}, u32[]{:S(2)}) %copy-start.1) | copy-done | bytes 1016600
  2.8 3.9 %shard_map.131 = (f32[8,4096]{1,0:T(8,128)S(1)}, f32[32,152,128]{2,1,0:T(8,128)S(1)}, f32[208,128]{1,0:T(8,128)S(1)}, f32[208,128]{1,0:T(8,128)S(1)}, s32[152,1]{1,0:T(8,128)S(1)}) custom-call(s32[1,1]{1,0:T(1,128)} %bitcast.odd_ref, s32[1,76]{1,0:T(1,128)S(1)} %bitcast.34, f32[1,4096]{1,0:T(1,128)S(1)} %bitcast.29, s32[1,4096]{1,0:T(1,128)S(1)} %bitcast.30, ...), custom_call_target="tpu_custom_call" | custom-call | flops 4000000000 | bytes 12000000 | tf_op jit(solution)/shard_map/pallas_call | solution.py:533
  6.7 5.9 %shard_map.132 = f32[2,4096]{1,0:T(2,128)S(1)} custom-call(f32[32,152,128]{2,1,0:T(8,128)S(1)} %get-tuple-element.34.phase_ref, f32[8,4096]{1,0:T(8,128)S(1)} %get-tuple-element.35.data_ref, s32[152,1]{1,0:T(8,128)S(1)} %get-tuple-element.36.order_ref, f32[76,2,304]{2,1,0:T(2,128)S(1)} %bitcast.19, f32[76,2,304]{2,1,0:T(2,128)S(1)} %bitcast.14, ...), custom_call_target="tpu_custom_call" | custom-call | flops 6000000000 | bytes 18000000 | tf_op jit(solution)/shard_map/pallas_call | solution.py:553
  13.2 2.6 %collective-permute-start.2 = (f32[208,128]{1,0:T(8,128)S(1)}, f32[208,128]{1,0:T(8,128)S(1)}, u32[]{:S(2)}, u32[]{:S(2)}) collective-permute-start(f32[208,128]{1,0:T(8,128)S(1)} %get-tuple-element.38), channel_id=1, source_target_pairs={{0,4},{4,0},{8,12},{12,8},{16,20},{20,16},{24,28},{28,24},{1,5},{5... | collective-permute-start | bytes 319496 | tf_op jit(solution)/shard_map/ppermute | solution.py:541
  16.5 1.6 %collective-permute-start.1 = (f32[2,4096]{1,0:T(2,128)S(1)}, f32[2,4096]{1,0:T(2,128)S(1)}, u32[]{:S(2)}, u32[]{:S(2)}) collective-permute-start(f32[2,4096]{1,0:T(2,128)S(1)} %add.50), channel_id=1, source_target_pairs={{0,2},{1,3},{2,0},{3,1},{4,6},{5,7},{6,4},{7,5},{8,10},{9,11},{10,... | collective-permute-start | bytes 98312 | tf_op jit(solution)/shard_map/ppermute | solution.py:490
  18.0 2.2 %shard_map.133.pre.refs_9_ = f32[19,152,304]{2,1,0:T(8,128)S(1)} custom-call(f32[19,76,2,304]{3,2,1,0:T(2,128)S(1)} %bitcast.28), custom_call_target="tpu_custom_call" | custom-call | flops 3000000000 | bytes 9000000 | tf_op jit(solution)/shard_map/pallas_call | solution.py:544
  20.5 2.3 %shard_map.134 = (f32[208,128]{1,0:T(8,128)S(1)}, f32[192,128]{1,0:T(8,128)S(1)}) custom-call(f32[2,4096]{1,0:T(2,128)S(1)} %add.51.p_ref.before_ref, f32[8,4096]{1,0:T(8,128)S(1)} %get-tuple-element.35.data_ref, f32[32,152,128]{2,1,0:T(8,128)S(1)} %get-tuple-element.34.phase_ref, f32[208,128]{1,0:T(8,128)S(1)} %collective-permute-done.2.pair_ref, ...), custom_call_target="tpu_custom_call" | custom-call | flops 2000000000 | bytes 6000000 | tf_op jit(solution)/shard_map/pallas_call | solution.py:558
  22.8 4.7 %collective-permute-start.7 = (f32[192,128]{1,0:T(8,128)S(1)}, f32[192,128]{1,0:T(8,128)S(1)}, u32[]{:S(2)}, u32[]{:S(2)}) collective-permute-start(f32[192,128]{1,0:T(8,128)S(1)} %get-tuple-element.45), channel_id=1, source_target_pairs={{0,8},{4,12},{8,0},{12,4},{16,24},{20,28},{24,16},{28,20},{1,9},{5... | collective-permute-start | bytes 294920 | tf_op jit(solution)/shard_map/ppermute | solution.py:490
  27.5 1.2 %collective-permute-start.4 = (f32[208,128]{1,0:T(8,128)S(1)}, f32[208,128]{1,0:T(8,128)S(1)}, u32[]{:S(2)}, u32[]{:S(2)}) collective-permute-start(f32[208,128]{1,0:T(8,128)S(1)} %get-tuple-element.40), channel_id=1, source_target_pairs={{0,4},{4,0},{8,12},{12,8},{16,20},{20,16},{24,28},{28,24},{1,5},{5... | collective-permute-start | bytes 319496 | tf_op jit(solution)/shard_map/ppermute | solution.py:490
  28.7 1.4 %collective-permute-done.7 = f32[192,128]{1,0:T(8,128)S(1)} collective-permute-done((f32[192,128]{1,0:T(8,128)S(1)}, f32[192,128]{1,0:T(8,128)S(1)}, u32[]{:S(2)}, u32[]{:S(2)}) %collective-permute-start.7) | collective-permute-done | bytes 98336 | tf_op jit(solution)/shard_map/ppermute | solution.py:490
  30.1 3.1 %collective-permute-start.8 = (f32[192,128]{1,0:T(8,128)S(1)}, f32[192,128]{1,0:T(8,128)S(1)}, u32[]{:S(2)}, u32[]{:S(2)}) collective-permute-start(f32[192,128]{1,0:T(8,128)S(1)} %add.55), channel_id=1, source_target_pairs={{0,16},{4,20},{8,24},{12,28},{16,0},{20,4},{24,8},{28,12},{1,17},{... | collective-permute-start | bytes 294920 | tf_op jit(solution)/shard_map/ppermute | solution.py:490
  33.3 1.6 %collective-permute-start.5 = (f32[208,128]{1,0:T(8,128)S(1)}, f32[208,128]{1,0:T(8,128)S(1)}, u32[]{:S(2)}, u32[]{:S(2)}) collective-permute-start(f32[208,128]{1,0:T(8,128)S(1)} %add.52), channel_id=1, source_target_pairs={{0,8},{4,12},{8,0},{12,4},{16,24},{20,28},{24,16},{28,20},{1,9},{5... | collective-permute-start | bytes 319496 | tf_op jit(solution)/shard_map/ppermute | solution.py:490
  36.0 1.5 %collective-permute-start.9 = (f32[192,128]{1,0:T(8,128)S(1)}, f32[192,128]{1,0:T(8,128)S(1)}, u32[]{:S(2)}, u32[]{:S(2)}) collective-permute-start(f32[192,128]{1,0:T(8,128)S(1)} %add.56), channel_id=1, source_target_pairs={{0,4},{4,0},{8,12},{12,8},{16,20},{20,16},{24,28},{28,24},{1,5},{5... | collective-permute-start | bytes 294920 | tf_op jit(solution)/shard_map/ppermute | solution.py:490
  38.1 2.1 %collective-permute-start.6 = (f32[208,128]{1,0:T(8,128)S(1)}, f32[208,128]{1,0:T(8,128)S(1)}, u32[]{:S(2)}, u32[]{:S(2)}) collective-permute-start(f32[208,128]{1,0:T(8,128)S(1)} %add.53), channel_id=1, source_target_pairs={{0,16},{4,20},{8,24},{12,28},{16,0},{20,4},{24,8},{28,12},{1,17},{... | collective-permute-start | bytes 319496 | tf_op jit(solution)/shard_map/ppermute | solution.py:490
  40.7 4.1 %shard_map.136 = (f32[144,160]{1,0:T(8,128)S(1)}, f32[1,128]{1,0:T(1,128)S(1)}, f32[72,304]{1,0:T(8,128)S(1)}, f32[72,304]{1,0:T(8,128)S(1)}, f32[72,304]{1,0:T(8,128)S(1)}, /*index=5*/f32[72,304]{1,0:T(8,128)S(1)}) custom-call(f32[192,128]{1,0:T(8,128)S(1)} %add.57.gathered_ref, s32[152,1]{1,0:T(8,128)S(1)} %get-tuple-element.36.order_ref, ...), custom_call_target="tpu_custom_call" | custom-call | flops 4000000000 | bytes 12000000 | tf_op jit(solution)/shard_map/pallas_call | solution.py:562
  44.8 4.5 %shard_map.135 = (f32[160,160]{1,0:T(8,128)S(1)}, f32[1,128]{1,0:T(1,128)S(1)}, f32[80,304]{1,0:T(8,128)S(1)}, f32[80,304]{1,0:T(8,128)S(1)}, f32[80,304]{1,0:T(8,128)S(1)}, /*index=5*/f32[80,304]{1,0:T(8,128)S(1)}) custom-call(f32[208,128]{1,0:T(8,128)S(1)} %add.54.gathered_ref, s32[152,1]{1,0:T(8,128)S(1)} %get-tuple-element.36.order_ref, ...), custom_call_target="tpu_custom_call" | custom-call | flops 4000000000 | bytes 12000000 | tf_op jit(solution)/shard_map/pallas_call | solution.py:562
  49.3 1.7 %shard_map.137 = f32[2,4224]{1,0:T(2,128)S(1)} custom-call(f32[160,160]{1,0:T(8,128)S(1)} %get-tuple-element.44.first_ref, f32[144,160]{1,0:T(8,128)S(1)} %get-tuple-element.46.second_ref, f32[1,128]{1,0:T(1,128)S(1)} %get-tuple-element.47.dots_a, f32[1,128]{1,0:T(1,128)S(1)} %get-tuple-element.48.dots_b, f32[32,152,128]{2,1,0:T(8,128)S(1)} %get-tuple-element.34.phase_ref, ...), custom_call_target="tpu_custom_call" | custom-call | flops 2000000000 | bytes 6000000 | tf_op jit(solution)/shard_map/pallas_call | solution.py:573
  51.1 1.2 %collective-permute-done.10 = f32[2,4224]{1,0:T(2,128)S(1)} collective-permute-done((f32[2,4224]{1,0:T(2,128)S(1)}, f32[2,4224]{1,0:T(2,128)S(1)}, u32[]{:S(2)}, u32[]{:S(2)}) %collective-permute-start.10) | collective-permute-done | bytes 33824 | tf_op jit(solution)/shard_map/ppermute | solution.py:490
  52.3 1.6 %collective-permute-start.11 = (f32[2,4224]{1,0:T(2,128)S(1)}, f32[2,4224]{1,0:T(2,128)S(1)}, u32[]{:S(2)}, u32[]{:S(2)}) collective-permute-start(f32[2,4224]{1,0:T(2,128)S(1)} %add.58), channel_id=1, source_target_pairs={{0,2},{1,3},{2,0},{3,1},{4,6},{5,7},{6,4},{7,5},{8,10},{9,11},{10,... | collective-permute-start | bytes 101384 | tf_op jit(solution)/shard_map/ppermute | solution.py:490
  53.9 2.4 %collective-permute-done.11 = f32[2,4224]{1,0:T(2,128)S(1)} collective-permute-done((f32[2,4224]{1,0:T(2,128)S(1)}, f32[2,4224]{1,0:T(2,128)S(1)}, u32[]{:S(2)}, u32[]{:S(2)}) %collective-permute-start.11) | collective-permute-done | bytes 33824 | tf_op jit(solution)/shard_map/ppermute | solution.py:490
  56.3 2.0 %shard_map.138 = f32[200,128]{1,0:T(8,128)S(1)} custom-call(f32[2,4224]{1,0:T(2,128)S(1)} %add.59.p_ref.row_ref, f32[2,4096]{1,0:T(2,128)S(1)} %add.51.p_ref.before_ref, f32[8,4096]{1,0:T(8,128)S(1)} %get-tuple-element.35.data_ref, f32[32,152,128]{2,1,0:T(8,128)S(1)} %get-tuple-element.34.phase_ref, f32[208,128]{1,0:T(8,128)S(1)} %collective-permute-done.2.pair_ref, ...), custom_call_target="tpu_custom_call" | custom-call | flops 2000000000 | bytes 6000000 | tf_op jit(solution)/shard_map/pallas_call | solution.py:577
  58.3 1.5 %collective-permute-start.12 = (f32[200,128]{1,0:T(8,128)S(1)}, f32[200,128]{1,0:T(8,128)S(1)}, u32[]{:S(2)}, u32[]{:S(2)}) collective-permute-start(f32[200,128]{1,0:T(8,128)S(1)} %shard_map.138), channel_id=1, source_target_pairs={{0,4},{4,0},{8,12},{12,8},{16,20},{20,16},{24,28},{28,24},{1,5},{5... | collective-permute-start | bytes 307208 | tf_op jit(solution)/shard_map/ppermute | solution.py:490
  59.8 3.2 %collective-permute-done.12 = f32[200,128]{1,0:T(8,128)S(1)} collective-permute-done((f32[200,128]{1,0:T(8,128)S(1)}, f32[200,128]{1,0:T(8,128)S(1)}, u32[]{:S(2)}, u32[]{:S(2)}) %collective-permute-start.12) | collective-permute-done | bytes 102432 | tf_op jit(solution)/shard_map/ppermute | solution.py:490
  63.1 2.0 %collective-permute-start.13 = (f32[200,128]{1,0:T(8,128)S(1)}, f32[200,128]{1,0:T(8,128)S(1)}, u32[]{:S(2)}, u32[]{:S(2)}) collective-permute-start(f32[200,128]{1,0:T(8,128)S(1)} %add.60), channel_id=1, source_target_pairs={{0,8},{4,12},{8,0},{12,4},{16,24},{20,28},{24,16},{28,20},{1,9},{5... | collective-permute-start | bytes 307208 | tf_op jit(solution)/shard_map/ppermute | solution.py:490
  65.1 2.7 %collective-permute-done.13 = f32[200,128]{1,0:T(8,128)S(1)} collective-permute-done((f32[200,128]{1,0:T(8,128)S(1)}, f32[200,128]{1,0:T(8,128)S(1)}, u32[]{:S(2)}, u32[]{:S(2)}) %collective-permute-start.13) | collective-permute-done | bytes 102432 | tf_op jit(solution)/shard_map/ppermute | solution.py:490
  67.8 3.7 %collective-permute-start.14 = (f32[200,128]{1,0:T(8,128)S(1)}, f32[200,128]{1,0:T(8,128)S(1)}, u32[]{:S(2)}, u32[]{:S(2)}) collective-permute-start(f32[200,128]{1,0:T(8,128)S(1)} %add.61), channel_id=1, source_target_pairs={{0,16},{4,20},{8,24},{12,28},{16,0},{20,4},{24,8},{28,12},{1,17},{... | collective-permute-start | bytes 307208 | tf_op jit(solution)/shard_map/ppermute | solution.py:490
  71.5 2.6 %collective-permute-done.14 = f32[200,128]{1,0:T(8,128)S(1)} collective-permute-done((f32[200,128]{1,0:T(8,128)S(1)}, f32[200,128]{1,0:T(8,128)S(1)}, u32[]{:S(2)}, u32[]{:S(2)}) %collective-permute-start.14) | collective-permute-done | bytes 102432 | tf_op jit(solution)/shard_map/ppermute | solution.py:490
  74.2 3.6 %shard_map.139 = (f32[1,128]{1,0:T(1,128)S(1)}, f32[152,304]{1,0:T(8,128)S(1)}, f32[152,304]{1,0:T(8,128)S(1)}) custom-call(f32[200,128]{1,0:T(8,128)S(1)} %add.62.gathered_ref, f32[2,4224]{1,0:T(2,128)S(1)} %add.59.p_ref.row_ref, s32[152,1]{1,0:T(8,128)S(1)} %get-tuple-element.36.order_ref, f32[76,2,304]{2,1,0:T(2,128)S(1)} %bitcast.25, ...), custom_call_target="tpu_custom_call" | custom-call | flops 4000000000 | bytes 12000000 | tf_op jit(solution)/shard_map/pallas_call | solution.py:581
  77.8 1.2 %collective-permute-done.15 = f32[1,128]{1,0:T(1,128)S(1)} collective-permute-done((f32[1,128]{1,0:T(1,128)S(1)}, f32[1,128]{1,0:T(1,128)S(1)}, u32[]{:S(2)}, u32[]{:S(2)}) %collective-permute-start.15) | collective-permute-done | bytes 544 | tf_op jit(solution)/shard_map/ppermute | solution.py:490
  79.0 1.5 %collective-permute-start.16 = (f32[1,128]{1,0:T(1,128)S(1)}, f32[1,128]{1,0:T(1,128)S(1)}, u32[]{:S(2)}, u32[]{:S(2)}) collective-permute-start(f32[1,128]{1,0:T(1,128)S(1)} %add.63), channel_id=1, source_target_pairs={{0,2},{1,3},{2,0},{3,1},{4,6},{5,7},{6,4},{7,5},{8,10},{9,11},{10,... | collective-permute-start | bytes 1544 | tf_op jit(solution)/shard_map/ppermute | solution.py:490
  80.4 2.1 %collective-permute-done.16 = f32[1,128]{1,0:T(1,128)S(1)} collective-permute-done((f32[1,128]{1,0:T(1,128)S(1)}, f32[1,128]{1,0:T(1,128)S(1)}, u32[]{:S(2)}, u32[]{:S(2)}) %collective-permute-start.16) | collective-permute-done | bytes 544 | tf_op jit(solution)/shard_map/ppermute | solution.py:490
  82.5 1.3 %shard_map.140 = (f32[76,2,304]{2,1,0:T(2,128)}, f32[76,2,304]{2,1,0:T(2,128)}, f32[76,2,304]{2,1,0:T(2,128)}) custom-call(f32[2,4224]{1,0:T(2,128)S(1)} %add.59.p_ref.row_ref, f32[1,128]{1,0:T(1,128)S(1)} %add.64.dots_ref, s32[152,1]{1,0:T(8,128)S(1)} %get-tuple-element.36.order_ref, f32[76,2,304]{2,1,0:T(2,128)S(1)} %bitcast.22, ...), custom_call_target="tpu_custom_call" | custom-call | tf_op jit(solution)/shard_map/pallas_call | solution.py:585
  (57 shorter events, 4.8 us)
Async XLA Ops:
  0.6 2.1 %copy-start.6 = (f32[4096]{0:T(1024)S(1)}, f32[4096]{0:T(1024)}, u32[]{:S(2)}) copy-start(f32[4096]{0:T(1024)} %param.11) | copy-start | bytes 49156
  0.6 2.0 %copy-start.7 = (s32[4096]{0:T(1024)S(1)}, s32[4096]{0:T(1024)}, u32[]{:S(2)}) copy-start(s32[4096]{0:T(1024)} %param.12) | copy-start | bytes 49156
  0.7 2.0 %copy-start.8 = (f32[4096]{0:T(1024)S(1)}, f32[4096]{0:T(1024)}, u32[]{:S(2)}) copy-start(f32[4096]{0:T(1024)} %param.13) | copy-start | bytes 49156
  0.7 2.0 %copy-start.9 = (s32[4096]{0:T(1024)S(1)}, s32[4096]{0:T(1024)}, u32[]{:S(2)}) copy-start(s32[4096]{0:T(1024)} %param.15) | copy-start | bytes 49156
  0.7 2.0 %copy-start.10 = (f32[4096]{0:T(1024)S(1)}, f32[4096]{0:T(1024)}, u32[]{:S(2)}) copy-start(f32[4096]{0:T(1024)} %param.14) | copy-start | bytes 49156
  0.7 2.0 %copy-start.11 = (s32[76]{0:T(128)S(1)}, s32[76]{0:T(128)}, u32[]{:S(2)}) copy-start(s32[76]{0:T(128)} %param.16) | copy-start | bytes 916
  1.5 1.2 %copy-start.1 = (bf16[19,152,176]{2,1,0:T(8,128)(2,1)}, bf16[19,152,176]{2,1,0:T(8,128)(2,1)S(1)}, u32[]{:S(2)}) copy-start(bf16[19,152,176]{2,1,0:T(8,128)(2,1)S(1)} %get-tuple-element.43.refs_2_.refs_12_) | copy-start | bytes 3049732
  2.7 3.9 %copy-start = (bf16[76,160,304]{2,1,0:T(8,128)(2,1)S(1)}, bf16[76,160,304]{2,1,0:T(8,128)(2,1)}, u32[]{:S(2)}) copy-start(bf16[76,160,304]{2,1,0:T(8,128)(2,1)} %refs_8_.1) | copy-start | bytes 22179844
  2.7 3.9 %copy-start.3 = (f32[2,76,304]{2,0,1:T(2,128)S(1)}, f32[2,76,304]{2,0,1:T(2,128)}, u32[]{:S(2)}) copy-start(f32[2,76,304]{2,0,1:T(2,128)} %param.21) | copy-start | bytes 554500
  2.8 3.9 %copy-start.4 = (f32[2,76,304]{2,0,1:T(2,128)S(1)}, f32[2,76,304]{2,0,1:T(2,128)}, u32[]{:S(2)}) copy-start(f32[2,76,304]{2,0,1:T(2,128)} %param.20) | copy-start | bytes 554500
  2.8 15.3 %slice-start = ((s8[4435968]{0:T(1024)(128)(4,1)}), s8[4194304]{0:T(1024)(128)(4,1)S(1)}, s32[]{:S(2)}) async-start(s8[4435968]{0:T(1024)(128)(4,1)} %bitcast.26), calls=%async_computation | async-start | bytes 8388608
  6.7 11.3 %slice-start.1 = ((s8[4435968]{0:T(1024)(128)(4,1)}), s8[241664]{0:T(1024)(128)(4,1)S(1)}, s32[]{:S(2)}) async-start(s8[4435968]{0:T(1024)(128)(4,1)} %bitcast.26), calls=%async_computation.1 | async-start | bytes 483328
  12.6 3.8 %collective-permute-start = (f32[2,4096]{1,0:T(2,128)S(1)}, f32[2,4096]{1,0:T(2,128)S(1)}, u32[]{:S(2)}, u32[]{:S(2)}) collective-permute-start(f32[2,4096]{1,0:T(2,128)S(1)} %shard_map.132), channel_id=1, source_target_pairs={{0,1},{1,0},{2,3},{3,2},{4,5},{5,4},{6,7},{7,6},{8,9},{9,8},{10,11... | collective-permute-start | bytes 98312 | tf_op jit(solution)/shard_map/ppermute | solution.py:490
  13.2 7.3 %collective-permute-start.2 = (f32[208,128]{1,0:T(8,128)S(1)}, f32[208,128]{1,0:T(8,128)S(1)}, u32[]{:S(2)}, u32[]{:S(2)}) collective-permute-start(f32[208,128]{1,0:T(8,128)S(1)} %get-tuple-element.38), channel_id=1, source_target_pairs={{0,4},{4,0},{8,12},{12,8},{16,20},{20,16},{24,28},{28,24},{1,5},{5... | collective-permute-start | bytes 319496 | tf_op jit(solution)/shard_map/ppermute | solution.py:541
  15.8 4.7 %collective-permute-start.3 = (f32[208,128]{1,0:T(8,128)S(1)}, f32[208,128]{1,0:T(8,128)S(1)}, u32[]{:S(2)}, u32[]{:S(2)}) collective-permute-start(f32[208,128]{1,0:T(8,128)S(1)} %get-tuple-element.39), channel_id=1, source_target_pairs={{4,8},{12,16},{20,24},{8,4},{16,12},{24,20},{5,9},{13,17},{21,25},... | collective-permute-start | bytes 319496 | tf_op jit(solution)/shard_map/ppermute | solution.py:543
  16.5 4.0 %collective-permute-start.1 = (f32[2,4096]{1,0:T(2,128)S(1)}, f32[2,4096]{1,0:T(2,128)S(1)}, u32[]{:S(2)}, u32[]{:S(2)}) collective-permute-start(f32[2,4096]{1,0:T(2,128)S(1)} %add.50), channel_id=1, source_target_pairs={{0,2},{1,3},{2,0},{3,1},{4,6},{5,7},{6,4},{7,5},{8,10},{9,11},{10,... | collective-permute-start | bytes 98312 | tf_op jit(solution)/shard_map/ppermute | solution.py:490
  20.5 20.2 %copy-start.5 = (f32[2,76,304]{2,0,1:T(2,128)S(1)}, f32[2,76,304]{2,0,1:T(2,128)}, u32[]{:S(2)}) copy-start(f32[2,76,304]{2,0,1:T(2,128)} %param.19) | copy-start | bytes 554500
  22.8 17.9 %copy-start.2 = (bf16[19,152,176]{2,1,0:T(8,128)(2,1)S(1)}, bf16[19,152,176]{2,1,0:T(8,128)(2,1)}, u32[]{:S(2)}) copy-start(bf16[19,152,176]{2,1,0:T(8,128)(2,1)} %copy-done.1) | copy-start | bytes 3049732
  22.8 7.3 %collective-permute-start.7 = (f32[192,128]{1,0:T(8,128)S(1)}, f32[192,128]{1,0:T(8,128)S(1)}, u32[]{:S(2)}, u32[]{:S(2)}) collective-permute-start(f32[192,128]{1,0:T(8,128)S(1)} %get-tuple-element.45), channel_id=1, source_target_pairs={{0,8},{4,12},{8,0},{12,4},{16,24},{20,28},{24,16},{28,20},{1,9},{5... | collective-permute-start | bytes 294920 | tf_op jit(solution)/shard_map/ppermute | solution.py:490
  27.5 5.7 %collective-permute-start.4 = (f32[208,128]{1,0:T(8,128)S(1)}, f32[208,128]{1,0:T(8,128)S(1)}, u32[]{:S(2)}, u32[]{:S(2)}) collective-permute-start(f32[208,128]{1,0:T(8,128)S(1)} %get-tuple-element.40), channel_id=1, source_target_pairs={{0,4},{4,0},{8,12},{12,8},{16,20},{20,16},{24,28},{28,24},{1,5},{5... | collective-permute-start | bytes 319496 | tf_op jit(solution)/shard_map/ppermute | solution.py:490
  30.1 5.8 %collective-permute-start.8 = (f32[192,128]{1,0:T(8,128)S(1)}, f32[192,128]{1,0:T(8,128)S(1)}, u32[]{:S(2)}, u32[]{:S(2)}) collective-permute-start(f32[192,128]{1,0:T(8,128)S(1)} %add.55), channel_id=1, source_target_pairs={{0,16},{4,20},{8,24},{12,28},{16,0},{20,4},{24,8},{28,12},{1,17},{... | collective-permute-start | bytes 294920 | tf_op jit(solution)/shard_map/ppermute | solution.py:490
  33.3 4.8 %collective-permute-start.5 = (f32[208,128]{1,0:T(8,128)S(1)}, f32[208,128]{1,0:T(8,128)S(1)}, u32[]{:S(2)}, u32[]{:S(2)}) collective-permute-start(f32[208,128]{1,0:T(8,128)S(1)} %add.52), channel_id=1, source_target_pairs={{0,8},{4,12},{8,0},{12,4},{16,24},{20,28},{24,16},{28,20},{1,9},{5... | collective-permute-start | bytes 319496 | tf_op jit(solution)/shard_map/ppermute | solution.py:490
  36.0 4.7 %collective-permute-start.9 = (f32[192,128]{1,0:T(8,128)S(1)}, f32[192,128]{1,0:T(8,128)S(1)}, u32[]{:S(2)}, u32[]{:S(2)}) collective-permute-start(f32[192,128]{1,0:T(8,128)S(1)} %add.56), channel_id=1, source_target_pairs={{0,4},{4,0},{8,12},{12,8},{16,20},{20,16},{24,28},{28,24},{1,5},{5... | collective-permute-start | bytes 294920 | tf_op jit(solution)/shard_map/ppermute | solution.py:490
  38.1 6.7 %collective-permute-start.6 = (f32[208,128]{1,0:T(8,128)S(1)}, f32[208,128]{1,0:T(8,128)S(1)}, u32[]{:S(2)}, u32[]{:S(2)}) collective-permute-start(f32[208,128]{1,0:T(8,128)S(1)} %add.53), channel_id=1, source_target_pairs={{0,16},{4,20},{8,24},{12,28},{16,0},{20,4},{24,8},{28,12},{1,17},{... | collective-permute-start | bytes 319496 | tf_op jit(solution)/shard_map/ppermute | solution.py:490
  51.0 1.3 %collective-permute-start.10 = (f32[2,4224]{1,0:T(2,128)S(1)}, f32[2,4224]{1,0:T(2,128)S(1)}, u32[]{:S(2)}, u32[]{:S(2)}) collective-permute-start(f32[2,4224]{1,0:T(2,128)S(1)} %shard_map.137), channel_id=1, source_target_pairs={{0,1},{1,0},{2,3},{3,2},{4,5},{5,4},{6,7},{7,6},{8,9},{9,8},{10,11... | collective-permute-start | bytes 101384 | tf_op jit(solution)/shard_map/ppermute | solution.py:490
  52.3 4.0 %collective-permute-start.11 = (f32[2,4224]{1,0:T(2,128)S(1)}, f32[2,4224]{1,0:T(2,128)S(1)}, u32[]{:S(2)}, u32[]{:S(2)}) collective-permute-start(f32[2,4224]{1,0:T(2,128)S(1)} %add.58), channel_id=1, source_target_pairs={{0,2},{1,3},{2,0},{3,1},{4,6},{5,7},{6,4},{7,5},{8,10},{9,11},{10,... | collective-permute-start | bytes 101384 | tf_op jit(solution)/shard_map/ppermute | solution.py:490
  58.3 4.7 %collective-permute-start.12 = (f32[200,128]{1,0:T(8,128)S(1)}, f32[200,128]{1,0:T(8,128)S(1)}, u32[]{:S(2)}, u32[]{:S(2)}) collective-permute-start(f32[200,128]{1,0:T(8,128)S(1)} %shard_map.138), channel_id=1, source_target_pairs={{0,4},{4,0},{8,12},{12,8},{16,20},{20,16},{24,28},{28,24},{1,5},{5... | collective-permute-start | bytes 307208 | tf_op jit(solution)/shard_map/ppermute | solution.py:490
  63.1 4.7 %collective-permute-start.13 = (f32[200,128]{1,0:T(8,128)S(1)}, f32[200,128]{1,0:T(8,128)S(1)}, u32[]{:S(2)}, u32[]{:S(2)}) collective-permute-start(f32[200,128]{1,0:T(8,128)S(1)} %add.60), channel_id=1, source_target_pairs={{0,8},{4,12},{8,0},{12,4},{16,24},{20,28},{24,16},{28,20},{1,9},{5... | collective-permute-start | bytes 307208 | tf_op jit(solution)/shard_map/ppermute | solution.py:490
  67.8 6.4 %collective-permute-start.14 = (f32[200,128]{1,0:T(8,128)S(1)}, f32[200,128]{1,0:T(8,128)S(1)}, u32[]{:S(2)}, u32[]{:S(2)}) collective-permute-start(f32[200,128]{1,0:T(8,128)S(1)} %add.61), channel_id=1, source_target_pairs={{0,16},{4,20},{8,24},{12,28},{16,0},{20,4},{24,8},{28,12},{1,17},{... | collective-permute-start | bytes 307208 | tf_op jit(solution)/shard_map/ppermute | solution.py:490
  77.8 1.2 %collective-permute-start.15 = (f32[1,128]{1,0:T(1,128)S(1)}, f32[1,128]{1,0:T(1,128)S(1)}, u32[]{:S(2)}, u32[]{:S(2)}) collective-permute-start(f32[1,128]{1,0:T(1,128)S(1)} %get-tuple-element.57), channel_id=1, source_target_pairs={{0,1},{1,0},{2,3},{3,2},{4,5},{5,4},{6,7},{7,6},{8,9},{9,8},{10,11... | collective-permute-start | bytes 1544 | tf_op jit(solution)/shard_map/ppermute | solution.py:490
  79.0 3.6 %collective-permute-start.16 = (f32[1,128]{1,0:T(1,128)S(1)}, f32[1,128]{1,0:T(1,128)S(1)}, u32[]{:S(2)}, u32[]{:S(2)}) collective-permute-start(f32[1,128]{1,0:T(1,128)S(1)} %add.63), channel_id=1, source_target_pairs={{0,2},{1,3},{2,0},{3,1},{4,6},{5,7},{6,4},{7,5},{8,10},{9,11},{10,... | collective-permute-start | bytes 1544 | tf_op jit(solution)/shard_map/ppermute | solution.py:490
